TPU v7x, 256 devices: a whole 4x4x8 slice. The times are simulated.
256 devices in a mesh: wave: 32 (over y, z), lev: 8 (over x, core).
Axes of the slice: x: 4, y: 4, z: 8, core: 2. Of those that a mesh axis runs over, the one named last changes fastest.
Arguments:
- fourier: float32 [2560, 24, 1088], P('wave', None, 'lev'), may hold values from -6 to 6
- weights: float32 [2560], P('wave'), may hold values from 0.3 to 3
- row_points: int32 [2560], replicated, may hold values from 20 to 5164, as said below
- slot_map: int32 [24], replicated, may hold values from 0 to 31, as said below
- legendre_lookup: float32 [32, 2, 640, 1280], P('wave'), may hold values from -0.15625 to 0.15625
- to_modes: float32 [136, 136], replicated, may hold values from -0.5 to 0.5
- from_modes: float32 [136, 136], replicated, may hold values from -0.5 to 0.5
- mode_rates: float32 [136], replicated, may hold values from 0.1 to 10
- thermal_response_matrix: float32 [136, 136], replicated, may hold values from -0.5 to 0.5
Outputs:
- spectra: float32 [32, 2, 640, 1088], P('wave', None, 'lev')
Inputs may be any that keep to these rules, and one draw needn't show every extreme that they name: `row_points`: row t has 20 + 4 * d + 4 * q points, d its distance in rows from the nearer pole and q a whole number from 0 to 7; row 1279, the last row of the northern hemisphere, reaches the largest value. `slot_map`: distinct global slots; slot s is held by device s of wave (one slot per device); which slots, and so which devices, hold a wavenumber is drawn from the seed.
All inputs are finite; a program needn't handle non-finite values.
Results may differ from a plain program's by a relative error of at most 0.0003.
Values sent between devices are 32-bit elements; how exact they have to be, the bound alone decides.
No kernel may reach another device: no remote copies, remote signals or barrier semaphores. Data moves between devices by JAX's collectives and lax.ppermute only.
A program may use at most 64 MiB of HBM per device.

v0:
```python
import jax
import jax.numpy as jnp
from jax import lax
from jax.sharding import PartitionSpec as P

NTRUNC = 1280
LEVELS = 136
FIELDS = 4


def vertical_step(spectra, degree, to_modes, from_modes, mode_rates, thermal_response_matrix):
    maximal_wave_truncation = lax.Precision.HIGHEST
    layerwise_coefficients = spectra.reshape(spectra.shape[:-1] + (LEVELS, FIELDS, 2))
    divergence = layerwise_coefficients[..., 1, :]
    modal = jnp.einsum("kl,...lc->...kc", to_modes, divergence, precision=maximal_wave_truncation)
    degrees = degree.astype(jnp.float32)
    wave_ratio = degrees * (degrees + 1.0) / (NTRUNC * NTRUNC)
    damping = 1.0 / (1.0 + mode_rates * wave_ratio[..., None])
    advanced_flow_spreading = jnp.einsum(
        "mc,...cb->...mb", from_modes, modal * damping[..., None], precision=maximal_wave_truncation
    )
    advanced_thermal_field = layerwise_coefficients[..., 2, :] - jnp.einsum(
        "mc,...cb->...mb",
        thermal_response_matrix,
        advanced_flow_spreading,
        precision=maximal_wave_truncation,
    )
    joined_coefficient_sets = jnp.stack(
        [
            layerwise_coefficients[..., 0, :],
            advanced_flow_spreading,
            advanced_thermal_field,
            layerwise_coefficients[..., 3, :],
        ],
        axis=-2,
    )
    return joined_coefficient_sets.reshape(spectra.shape)


def legendre_sums(paired, tables):
    maximal_wave_truncation = lax.Precision.HIGHEST
    return jnp.einsum("spih,phsc->spic", tables, paired, precision=maximal_wave_truncation)


def on_device(
    fourier,
    weights,
    row_points,
    slot_map,
    legendre_lookup,
    to_modes,
    from_modes,
    mode_rates,
    thermal_response_matrix,
):
    wave_count = lax.axis_size("wave")
    layer_number = lax.axis_size("lev")
    wave_index = lax.axis_index("wave")
    level_index = lax.axis_index("lev")
    lat_local = fourier.shape[0]
    window = fourier.shape[1]
    columns = fourier.shape[2]
    slot_count = legendre_lookup.shape[0]
    half_rows = legendre_lookup.shape[2]
    lat_half = legendre_lookup.shape[3]
    all_slots = slot_count * wave_count
    lat_total = 2 * lat_half
    stride = NTRUNC // window
    wavenum = jnp.arange(window, dtype=jnp.int32) * stride
    points_here = lax.dynamic_slice_in_dim(row_points, wave_index * lat_local, lat_local, 0)
    retained = (2 * wavenum[None, :] < points_here[:, None]).astype(jnp.float32)
    weighted = fourier * (weights[:, None] * retained)[:, :, None]
    slot_ids = jnp.arange(all_slots, dtype=jnp.int32)
    matches = (slot_map[None, :] == slot_ids[:, None]).astype(jnp.int32)
    used_all = jnp.sum(matches, axis=1)
    source_all = jnp.sum(matches * jnp.arange(window, dtype=jnp.int32)[None, :], axis=1)
    outgoing = jnp.take(weighted, source_all, axis=1) * used_all.astype(jnp.float32)[None, :, None]
    outgoing = outgoing.reshape(lat_local, wave_count, slot_count, columns)
    arrived = lax.all_to_all(outgoing, "wave", split_axis=1, concat_axis=0, tiled=True)
    arrived = arrived.reshape(lat_total, slot_count, columns)
    northern = arrived[:lat_half]
    southern = arrived[lat_half:][::-1]
    paired = jnp.stack([northern + southern, northern - southern])
    owned_orders = lax.dynamic_slice_in_dim(source_all, wave_index * slot_count, slot_count, 0)
    degree_base = owned_orders * stride
    row_count = half_rows // layer_number
    row_start = level_index * row_count
    local_spectra = legendre_sums(paired, legendre_lookup)
    spectra = lax.all_to_all(local_spectra, "lev", split_axis=2, concat_axis=3, tiled=True)
    row_ids = row_start + jnp.arange(row_count, dtype=jnp.int32)
    parities = jnp.arange(2, dtype=jnp.int32)
    degree = degree_base[:, None, None] + 2 * row_ids[None, None, :] + parities[None, :, None]
    validity = (degree < NTRUNC).astype(jnp.float32)
    joined_coefficient_sets = vertical_step(
        spectra, degree, to_modes, from_modes, mode_rates, thermal_response_matrix
    )
    return joined_coefficient_sets * validity[..., None]


def solution(mesh):
    placed = (
        P("wave", None, "lev"),
        P("wave"),
        P(),
        P(),
        P("wave", None, None, None),
        P(),
        P(),
        P(),
        P(),
    )
    return jax.shard_map(
        on_device,
        mesh=mesh,
        in_specs=placed,
        out_specs=P("wave", None, "lev", None),
        check_vma=False,
    )
```

profile of v0, /device:TPU:1, one launch (start us, length us, event | category | flops | bytes accessed | tf_op | source)
XLA Modules:
  0.0 122.7 jit_solution(361478988518212570)
XLA Ops:
  0.0 0.0 copy-start
  0.0 0.8 convert_reduce_fusion
  0.8 0.8 dynamic_slice.6
  1.6 0.7 compare_select_fusion
  2.3 1.6 %broadcast_multiply_fusion = f32[80,24,136]{0,2,1:T(8,128)S(1)} fusion(f32[80,24,136]{0,2,1:T(8,128)} %param.9, f32[80,24]{0,1:T(8,128)S(1)} %compare_select_fusion), kind=kLoop, calls=%fused_computation.16 | loop fusion | flops 261120 | bytes 2096640 | tf_op jit(solution)/shard_map/mul | solution.py:72
  3.9 2.1 %gather_fusion = f32[32,80,136]{1,2,0:T(8,128)} fusion(f32[80,24,136]{0,2,1:T(8,128)S(1)} %broadcast_multiply_fusion, s32[1024]{0:T(1024)S(1)} %pad_clamp_fusion), kind=kCustom, calls=%fused_computation | custom fusion | bytes 2785408 | tf_op jit(solution)/shard_map/jit(_take)/gather | solution.py:77
  6.0 3.3 %fusion.2 = f32[80,32,1,136]{0,3,2,1:T(8,128)} fusion(f32[32,80,136]{1,2,0:T(8,128)} %gather_fusion, f32[32]{0:T(128)S(1)} %convert_element_type.30, pred[32]{0:T(512)(128)(4,1)S(1)} %compare_and_fusion), kind=kLoop, calls=%fused_computation.4 | loop fusion | flops 696320 | bytes 2785440 | tf_op jit(solution)/shard_map/mul | solution.py:77
  9.3 12.0 %all-to-all-start = ((f32[80,32,1,136]{0,3,2,1:T(8,128)}), f32[80,32,1,136]{0,3,2,1:T(8,128)S(1)}, u32[]{:S(2)}, u32[]{:S(2)}) async-start(f32[80,32,1,136]{0,3,2,1:T(8,128)} %fusion.2), calls=%async_computation | async-start | bytes 4456448 | tf_op jit(solution)/shard_map/all_to_all | solution.py:79
  21.3 0.6 dynamic_slice.7
  22.6 50.3 %all-to-all-done = f32[80,32,1,136]{0,3,2,1:T(8,128)S(1)} async-done(((f32[80,32,1,136]{0,3,2,1:T(8,128)}), f32[80,32,1,136]{0,3,2,1:T(8,128)S(1)}, u32[]{:S(2)}, u32[]{:S(2)}) %all-to-all-start) | async-done | bytes 1392672 | tf_op jit(solution)/shard_map/all_to_all | solution.py:79
  72.8 0.1 fusion.20
  73.0 0.2 copy.46
  73.2 0.5 slice.27
  73.7 7.1 %rev.3 = f32[1280,1,136]{0,2,1:T(8,128)} reverse(f32[1280,1,136]{0,2,1:T(8,128)S(1)} %slice.27), dimensions={0} | reverse | bytes 1392640 | tf_op jit(solution)/shard_map/rev | solution.py:82
  80.8 0.2 copy.45
  81.1 0.0 copy-start.1
  81.1 0.5 slice.25
  81.6 0.6 copy-done.1
  82.2 0.2 add_bitcast_fusion
  82.3 7.9 %fusion.5 = f32[1,2,640,136]{2,3,1,0:T(8,128)S(1)} fusion(f32[1,2,640,1280]{3,2,1,0:T(8,128)} %param.13, f32[1,1280,1,136]{1,3,0,2:T(8,128)S(1)} %get-tuple-element.10, f32[1,1280,1,136]{1,3,0,2:T(8,128)S(1)} %get-tuple-element.9), kind=kOutput, calls=%fused_computation.8 | convolution fusion | flops 2674216960 | bytes 8642560 | tf_op jit(solution)/shard_map/spih,phsc->spic/dot_general | solution.py:42
  90.2 2.0 %copy.48 = f32[1,2,640,136]{3,1,0,2:T(2,128)} copy(f32[1,2,640,136]{2,3,1,0:T(8,128)S(1)} %fusion.5) | data formatting | bytes 1392640 | tf_op jit(solution)/shard_map/spih,phsc->spic/dot_general | solution.py:42
  92.3 0.0 copy-start.4
  92.3 6.6 %all-to-all-start.1 = ((f32[1,2,640,136]{3,1,0,2:T(2,128)}), f32[1,2,640,136]{3,1,0,2:T(2,128)S(1)}, u32[]{:S(2)}, u32[]{:S(2)}) async-start(f32[1,2,640,136]{3,1,0,2:T(2,128)} %copy.48), calls=%async_computation.1 | async-start | bytes 2621440 | tf_op jit(solution)/shard_map/all_to_all | solution.py:89
  98.9 0.0 copy-done.4
  98.9 0.1 add_divide_fusion
  99.0 17.6 %all-to-all-done.1 = f32[1,2,640,136]{3,1,0,2:T(2,128)S(1)} async-done(((f32[1,2,640,136]{3,1,0,2:T(2,128)}), f32[1,2,640,136]{3,1,0,2:T(2,128)S(1)}, u32[]{:S(2)}, u32[]{:S(2)}) %all-to-all-start.1) | async-done | bytes 696352 | tf_op jit(solution)/shard_map/all_to_all | solution.py:89
  116.6 1.9 %copy.61 = f32[1,2,8,80,136]{3,4,2,1,0:T(8,128)S(1)} copy(f32[1,2,8,80,136]{4,1,3,2,0:T(2,128)S(1)} %bitcast.101) | data formatting | bytes 1392640 | tf_op jit(solution)/shard_map/all_to_all | solution.py:89
  118.6 0.4 fusion.21
  118.9 0.0 copy-start.2
  119.0 0.0 copy-start.3
  119.0 0.0 copy-done
  119.0 0.4 fusion.9
  119.5 0.4 copy-done.2
  119.9 0.4 fusion.14
  120.3 0.0 copy-done.3
  120.3 0.4 fusion.11
  120.7 0.1 pad_maximum_fusion
  120.8 0.6 copy.55
  121.4 0.1 broadcast_multiply_fusion.1
  121.5 1.2 copy.56
  (10 shorter events, 0.1 us)
Async XLA Ops:
  0.0 119.0 %copy-start = (f32[136,136]{1,0:T(8,128)S(1)}, f32[136,136]{1,0:T(8,128)}, u32[]{:S(2)}) copy-start(f32[136,136]{1,0:T(8,128)} %param.14) | copy-start | bytes 221956
  9.3 63.6 %all-to-all-start = ((f32[80,32,1,136]{0,3,2,1:T(8,128)}), f32[80,32,1,136]{0,3,2,1:T(8,128)S(1)}, u32[]{:S(2)}, u32[]{:S(2)}) async-start(f32[80,32,1,136]{0,3,2,1:T(8,128)} %fusion.2), calls=%async_computation | async-start | bytes 4456448 | tf_op jit(solution)/shard_map/all_to_all | solution.py:79
  81.1 1.1 copy-start.1
  92.3 6.6 %copy-start.4 = (f32[136]{0:T(256)S(1)}, f32[136]{0:T(256)}, u32[]{:S(2)}) copy-start(f32[136]{0:T(256)} %param.16) | copy-start | bytes 1636
  92.3 24.4 %all-to-all-start.1 = ((f32[1,2,640,136]{3,1,0,2:T(2,128)}), f32[1,2,640,136]{3,1,0,2:T(2,128)S(1)}, u32[]{:S(2)}, u32[]{:S(2)}) async-start(f32[1,2,640,136]{3,1,0,2:T(2,128)} %copy.48), calls=%async_computation.1 | async-start | bytes 2621440 | tf_op jit(solution)/shard_map/all_to_all | solution.py:89
  118.9 0.9 copy-start.2
  119.0 1.3 %copy-start.3 = (f32[136,136]{1,0:T(8,128)S(1)}, f32[136,136]{1,0:T(8,128)}, u32[]{:S(2)}) copy-start(f32[136,136]{1,0:T(8,128)} %param.17) | copy-start | bytes 221956
where the time goes:
time: 123 us
  waiting for transfers between devices  67.9 us (55%)
  local copies, waits for them, and re-layouts  19.3 us (16%)
  starting transfers between devices  18.6 us (15%)
  matrix products  9.13 us (7%)
  other arithmetic  6.82 us (6%)
    all_to_all x1, waiting for transfers between devices, on_device(): lax.all_to_all(outgoing, 'wave', split_axis=1, concat_axis=0, tiled=True)  50.3 us
    all_to_all x1, waiting for transfers between devices, on_device(): lax.all_to_all(local_spectra, 'lev', split_axis=2, concat_axis=3, tiled=T...  17.6 us
    all_to_all x1, starting transfers between devices, on_device(): lax.all_to_all(outgoing, 'wave', split_axis=1, concat_axis=0, tiled=True)  12 us
    dot_general x1, matrix products, legendre_sums(): jnp.einsum('spih,phsc->spic', tables, paired, precision=maximal_wave_trun...  7.9 us
    rev x1, local copies, waits for them, and re-layouts, on_device(): southern = arrived[lat_half:][::-1]  7.12 us
    all_to_all x1, starting transfers between devices, on_device(): lax.all_to_all(local_spectra, 'lev', split_axis=2, concat_axis=3, tiled=T...  6.58 us
    mul x1, other arithmetic, on_device(): jnp.take(weighted, source_all, axis=1)  3.29 us
  transfers between devices with their start and end apart: 2, of which 2 were waited for; matrix products, arithmetic and copies ran while one was open for 1% of the time, Pallas kernels for 0%

commit v1 on v0

v1 whole, which is shorter than its diff:
```python
import jax
import jax.numpy as jnp
from jax import lax
from jax.experimental import pallas as pl
from jax.experimental.pallas import tpu as pltpu
from jax.sharding import PartitionSpec as P

NTRUNC = 1280
LEVELS = 136
HALF = 64
F32 = jnp.float32
BF16 = jnp.bfloat16
VMEM = pltpu.VMEM


def whole():
    return pl.BlockSpec(memory_space=VMEM)


def smem():
    return pl.BlockSpec(memory_space=pltpu.SMEM)


def params(mb):
    return pltpu.CompilerParams(vmem_limit_bytes=mb << 20)


def lanes_of(shape):
    return lax.broadcasted_iota(jnp.int32, shape, 1)


def split(x):
    high = x.astype(BF16)
    low = (x - high.astype(F32)).astype(BF16)
    return high, low


def table_kernel(table_ref, out_ref):
    high, low = split(table_ref[0])
    out_ref[0, 0] = high
    out_ref[0, 1] = low


def split_table(table):
    parities, rows, lats = table.shape
    step = rows // 4
    return pl.pallas_call(
        table_kernel,
        out_shape=jax.ShapeDtypeStruct((parities, 2, rows, lats), BF16),
        grid=(parities, rows // step),
        in_specs=[pl.BlockSpec((1, step, lats), lambda p, r: (p, r, 0))],
        out_specs=pl.BlockSpec((1, 2, step, lats), lambda p, r: (p, 0, r, 0)),
        compiler_params=params(16),
        name="split_table",
    )(table)


def pack_kernel(slots, lat, stride, where_ref, map_ref, points_ref, weights_ref, x_ref, out_ref, order):
    window = x_ref.shape[0]
    w = where_ref[0]

    @pl.loop(0, slots)
    def _(s):
        order[s] = -1

    @pl.loop(0, window)
    def _(j):
        order[map_ref[j]] = j

    first = w * lat
    row = first // 128
    off = first - row * 128
    lane = lanes_of((1, 128))
    back = lax.rem(128 - off, 128)
    here = pltpu.roll(points_ref[pl.ds(row, 1), :], back, 1)
    after = pltpu.roll(points_ref[pl.ds(jnp.minimum(row + 1, points_ref.shape[0] - 1), 1), :], back, 1)
    points = jnp.where(lane < 128 - off, here, after)[:, :lat]
    weights = weights_ref[...]

    @pl.loop(0, slots)
    def _(s):
        j = order[s]
        jj = jnp.maximum(j, 0)
        live = (2 * stride * jj < points) & (j >= 0)
        scale = jnp.where(live, weights, 0.0)
        x = x_ref[jj] * scale
        y = jnp.transpose(x[:128])
        u, v = y[: lat // 2], y[lat // 2 :]
        left = lanes_of(u.shape) < HALF
        out_ref[s, 0:40, :] = jnp.where(left, u, pltpu.roll(v, HALF, 1))
        out_ref[s, 40:80, :] = jnp.where(left, pltpu.roll(u, HALF, 1), v)
        out_ref[s, 80:88, :] = jnp.zeros((8, 128), F32)
        out_ref[s, 80:88, :lat] = x[128:]


def pack(where, slot_map, points, weights, x, slots, stride):
    lat = x.shape[2]
    return pl.pallas_call(
        lambda *refs: pack_kernel(slots, lat, stride, *refs),
        out_shape=jax.ShapeDtypeStruct((slots, 88, 128), F32),
        in_specs=[smem(), smem(), whole(), whole(), whole()],
        out_specs=whole(),
        scratch_shapes=[pltpu.SMEM((slots,), jnp.int32)],
        compiler_params=params(24),
        name="pack",
    )(where, slot_map, points, weights, x)


def flip_rows(x):
    rows = lax.broadcasted_iota(jnp.int32, (8, 128), 0)
    tiles = [
        jnp.take_along_axis(x[8 * t : 8 * t + 8], 7 - rows, axis=0) for t in reversed(range(x.shape[0] // 8))
    ]
    return jnp.concatenate(tiles, axis=0)


def pair_main(north, south):
    other = pltpu.roll(flip_rows(south), HALF, 1)
    return north + other, north - other


def high_low(x):
    high = x.astype(BF16).astype(F32)
    return high, x - high


def store_main(dst, p, w, packed):
    high, low = high_low(packed)
    left = lanes_of(high.shape) < HALF
    dst[p, pl.ds(80 * w, 40), 0:128] = jnp.where(left, high, pltpu.roll(low, HALF, 1))
    dst[p, pl.ds(80 * w + 40, 40), 0:128] = jnp.where(left, pltpu.roll(high, HALF, 1), low)


def fold(t, shift):
    return t + pltpu.roll(t, 128 - shift, 1)


def products(table_ref, rhs, p):
    o = jnp.dot(table_ref[p], rhs[p].astype(BF16), preferred_element_type=F32)
    half = o.shape[0] // 2
    return o[:half] + o[half:]


def legendre_a_kernel(row0, x_ref, table_ref, out_ref, rhs):
    blocks = x_ref.shape[0]

    @pl.loop(0, blocks // 2)
    def _(w):
        for p, v in enumerate(pair_main(x_ref[w, pl.ds(row0, 40), :], x_ref[blocks - 1 - w, pl.ds(row0, 40), :])):
            store_main(rhs, p, w, v)

    even = fold(products(table_ref, rhs, 0), HALF)
    odd = fold(products(table_ref, rhs, 1), HALF)
    res = jnp.where(lanes_of(even.shape) < HALF, even, odd)
    out_ref[...] = res.reshape(out_ref.shape)


def legendre_a(x, table, members):
    rows = table.shape[1] // 2
    return pl.pallas_call(
        lambda *refs: legendre_a_kernel(0, *refs),
        out_shape=jax.ShapeDtypeStruct((members, rows // members, 128), F32),
        in_specs=[whole(), whole()],
        out_specs=whole(),
        scratch_shapes=[VMEM((2, table.shape[2], 128), F32)],
        compiler_params=params(40),
        name="legendre_a",
    )(x, table)


def legendre_b_kernel(row0, x_ref, table_ref, out_ref, rhs):
    blocks = x_ref.shape[0]
    half = blocks // 2
    members = out_ref.shape[0]
    lane80 = lanes_of((80, 128))
    zn = jnp.transpose(x_ref[0:half, row0 + 40 : row0 + 48, :].reshape(8 * half, 128))[:80]
    zs = flip_rows(jnp.transpose(x_ref[half:, row0 + 40 : row0 + 48, :].reshape(8 * half, 128))[:80])
    for w in range(half):
        n = pltpu.roll(zn, (128 - 8 * w) % 128, 1)
        s = pltpu.roll(zs, (128 - 8 * (half - 1 - w)) % 128, 1)
        for p, v in enumerate((n + s, n - s)):
            high, low = high_low(v)
            q = jnp.where(lane80 < 8, high, pltpu.roll(low, 8, 1))
            rhs[p, 80 * w : 80 * w + 80, 128:256] = jnp.where(lane80 < 16, q, 0.0)

    @pl.loop(0, half)
    def _(w):
        for p, v in enumerate(pair_main(x_ref[w, pl.ds(row0, 40), :], x_ref[blocks - 1 - w, pl.ds(row0, 40), :])):
            store_main(rhs, p, w, v)

    even = products(table_ref, rhs, 0)
    odd = products(table_ref, rhs, 1)
    e, o = fold(even[:, :128], HALF), fold(odd[:, :128], HALF)
    res = jnp.where(lanes_of(e.shape) < HALF, e, o)
    out_ref[:, 0:80, :] = res.reshape(members, 80, 128)
    ee, oo = fold(even[:, 128:], 8), fold(odd[:, 128:], 8)
    extra = jnp.where(lanes_of(ee.shape) < 8, ee, pltpu.roll(oo, 8, 1)).reshape(members, 80, 128)
    for k in range(members):
        padded = jnp.concatenate([extra[k], jnp.zeros((48, 128), F32)], axis=0)
        out_ref[k, 80:96, :] = jnp.transpose(padded)[:16]


def legendre_b(x, table, members):
    rows = table.shape[1] // 2
    return pl.pallas_call(
        lambda *refs: legendre_b_kernel(40, *refs),
        out_shape=jax.ShapeDtypeStruct((members, rows // members + 16, 128), F32),
        in_specs=[whole(), whole()],
        out_specs=whole(),
        scratch_shapes=[VMEM((2, table.shape[2], 256), F32)],
        compiler_params=params(40),
        name="legendre_b",
    )(x, table)


def dot3(a, b):
    ah, al = split(a)
    bh, bl = split(b)
    d = lambda u, v: jnp.dot(u, v, preferred_element_type=F32)
    return d(ah, bh) + (d(ah, bl) + d(al, bh))


def vertical_kernel(base_ref, to_ref, from_ref, thermal_ref, rates_ref, x_ref, out_ref, y):
    members = x_ref.shape[0]
    base = base_ref[0]
    row0 = base_ref[1]
    lane = lanes_of((1, 128))
    degree = [base + 2 * (row0 + lane) + p for p in range(2)]
    live = [(d < NTRUNC) & (lane < 80) for d in degree]
    pad = jnp.zeros((48, 128), F32)
    for l in range(members):
        a = jnp.transpose(jnp.concatenate([x_ref[l, 0:80, :], pad], axis=0))
        b = jnp.transpose(jnp.concatenate([x_ref[l, 80:160, :], pad], axis=0))
        e = x_ref[l, 160:176, :]
        for p in range(2):
            y[p, 136 * l : 136 * l + 64, :] = jnp.where(live[p], a[64 * p : 64 * p + 64], 0.0)
            y[p, 136 * l + 64 : 136 * l + 128, :] = jnp.where(live[p], b[64 * p : 64 * p + 64], 0.0)
            y[p, 136 * l + 128 : 136 * l + 136, :] = jnp.where(live[p], e[8 * p : 8 * p + 8], 0.0)
    div = jnp.concatenate(
        [y[p, pl.ds(2 + part, LEVELS, stride=8), :] for p in range(2) for part in range(2)], axis=1
    )
    modal = dot3(to_ref[...], div)
    damp = []
    for p in range(2):
        d = degree[p].astype(F32)
        ratio = d * (d + 1.0) / (NTRUNC * NTRUNC)
        damp.append(1.0 / (1.0 + rates_ref[...] * ratio))
    damped = modal * jnp.concatenate([damp[0], damp[0], damp[1], damp[1]], axis=1)
    new = dot3(from_ref[...], damped)
    heat = dot3(thermal_ref[...], new)
    for p in range(2):
        for part in range(2):
            at = 128 * (2 * p + part)
            y[p, pl.ds(2 + part, LEVELS, stride=8), :] = new[:, at : at + 128]
            t = y[p, pl.ds(4 + part, LEVELS, stride=8), :]
            y[p, pl.ds(4 + part, LEVELS, stride=8), :] = t - heat[:, at : at + 128]
    for p in range(2):
        for c in range(8):
            out_ref[p, :, 128 * c : 128 * c + 128] = jnp.transpose(y[p, 128 * c : 128 * c + 128, :])[:80]
        tail = jnp.concatenate([y[p, 1024:1088, :], jnp.zeros((64, 128), F32)], axis=0)
        out_ref[p, :, 1024:1088] = jnp.transpose(tail)[:80, :64]


def vertical(base, to_modes, from_modes, thermal, rates, x):
    return pl.pallas_call(
        vertical_kernel,
        out_shape=jax.ShapeDtypeStruct((2, 80, 8 * LEVELS), F32),
        in_specs=[smem()] + [whole()] * 5,
        out_specs=whole(),
        scratch_shapes=[VMEM((2, 8 * LEVELS, 128), F32)],
        compiler_params=params(24),
        name="vertical",
    )(base, to_modes, from_modes, thermal, rates, x)


def on_device(
    fourier,
    weights,
    row_points,
    slot_map,
    legendre_lookup,
    to_modes,
    from_modes,
    mode_rates,
    thermal_response_matrix,
):
    slots = lax.axis_size("wave")
    members = lax.axis_size("lev")
    w = lax.axis_index("wave")
    l = lax.axis_index("lev")
    lat, window, _ = fourier.shape
    stride = NTRUNC // window
    table = split_table(legendre_lookup[0])
    table = table.reshape(2, 1280, 1280)
    x = jnp.transpose(fourier, (1, 2, 0))
    packed = pack(
        w.reshape(1), slot_map, row_points.reshape(-1, 128), weights.reshape(1, lat), x, slots, stride
    )
    arrived = lax.all_to_all(packed, "wave", split_axis=0, concat_axis=0, tiled=True)
    a = legendre_a(arrived, table, members)
    b = legendre_b(arrived, table, members)
    local = jnp.concatenate([a, b], axis=1)
    mine = lax.all_to_all(local, "lev", split_axis=0, concat_axis=0, tiled=True)
    degree_base = stride * jnp.sum(jnp.where(slot_map == w, jnp.arange(window, dtype=jnp.int32), 0))
    base = jnp.stack([degree_base, l * 80]).astype(jnp.int32)
    out = vertical(base, to_modes, from_modes, thermal_response_matrix, mode_rates.reshape(-1, 1), mine)
    return out[None]


def solution(mesh):
    placed = (
        P("wave", None, "lev"),
        P("wave"),
        P(),
        P(),
        P("wave", None, None, None),
        P(),
        P(),
        P(),
        P(),
    )
    return jax.shard_map(
        on_device,
        mesh=mesh,
        in_specs=placed,
        out_specs=P("wave", None, "lev", None),
        check_vma=False,
    )
```

time: 123 us -> 94.4 us (0.77)
  waiting for transfers between devices: 67.9 us -> 37 us
  Pallas kernels: 0 us -> 22.6 us
  matrix products: 9.13 us -> 0 us
  local copies, waits for them, and re-layouts: 19.3 us -> 12 us
  other arithmetic: 6.82 us -> 1.65 us
  starting transfers between devices: 18.6 us -> 19.9 us
    all_to_all x2, waiting for transfers between devices: 67.9 us -> 37 us  [the longest x1 27.1 us: on_device(): lax.all_to_all(packed, 'wave', split_axis=0, concat_axis=0, tiled=True)]
    pallas_call x0 -> x5, Pallas kernels: none -> 22.6 us  [the longest x1 7.33 us: pack(): pl.pallas_call(lambda *refs: pack_kernel(slots, lat, stride, *refs), out_...]
    unnamed x12 -> x24, local copies, waits for them, and re-layouts: 1.06 us -> 11.9 us
    dot_general x4 -> x0, matrix products: 9.13 us -> none  [the longest x1 7.9 us: legendre_sums(): jnp.einsum('spih,phsc->spic', tables, paired, precision=maximal_wave_trun...]
    rev x1 -> x0, local copies, waits for them, and re-layouts: 7.12 us -> none  [on_device(): southern = arrived[lat_half:][::-1]]
    mul x5 -> x0, other arithmetic: 5.67 us -> none  [the longest x1 3.29 us: on_device(): jnp.take(weighted, source_all, axis=1)]
    gather x1 -> x0, local copies, waits for them, and re-layouts: 2.07 us -> none  [on_device(): jnp.take(weighted, source_all, axis=1)]
    dot_general x1 -> x0, local copies, waits for them, and re-layouts: 2.01 us -> none  [legendre_sums(): jnp.einsum('spih,phsc->spic', tables, paired, precision=maximal_wave_trun...]
  transfers between devices with their start and end apart: 2 -> 2, of which waited for: 2 -> 2; matrix products, arithmetic and copies ran while one was open for 1% -> 1% of each run, Pallas kernels for 0% -> 1%
where the time goes in v1:
time: 94.4 us; the launch traced here: 93.9 us
  waiting for transfers between devices  37 us (39%)
  Pallas kernels  22.6 us (24%)
  starting transfers between devices  19.9 us (21%)
  local copies, waits for them, and re-layouts  12 us (13%)
  other arithmetic  1.65 us (2%)
    all_to_all x1, waiting for transfers between devices, on_device(): lax.all_to_all(packed, 'wave', split_axis=0, concat_axis=0, tiled=True)  27.1 us
    all_to_all x1, starting transfers between devices, on_device(): lax.all_to_all(packed, 'wave', split_axis=0, concat_axis=0, tiled=True)  12 us
    unnamed x24, local copies, waits for them, and re-layouts  11.9 us
    all_to_all x1, waiting for transfers between devices, on_device(): mine = lax.all_to_all(local, 'lev', split_axis=0, concat_axis=0, tiled=True)  9.95 us
    all_to_all x1, starting transfers between devices, on_device(): mine = lax.all_to_all(local, 'lev', split_axis=0, concat_axis=0, tiled=True)  7.92 us
    pallas_call x1, Pallas kernels, pack(): pl.pallas_call(lambda *refs: pack_kernel(slots, lat, stride, *refs), out_...  7.33 us
    pallas_call x1, Pallas kernels, legendre_b(): pl.pallas_call(lambda *refs: legendre_b_kernel(40, *refs), out_shape=jax....  6.44 us
    pallas_call x1, Pallas kernels, legendre_a(): pl.pallas_call(lambda *refs: legendre_a_kernel(0, *refs), out_shape=jax.S...  4.49 us
  transfers between devices with their start and end apart: 2, of which 2 were waited for; matrix products, arithmetic and copies ran while one was open for 1% of the time, Pallas kernels for 1%

profile of v1, /device:TPU:1, one launch (start us, length us, event | category | flops | bytes accessed | tf_op | source)
XLA Modules:
  0.0 93.9 jit_solution(2155344767658046232)
XLA Ops:
  0.0 0.0 copy-start.3
  0.0 1.4 %copy-done.3 = f32[80,24,136]{0,2,1:T(8,128)S(1)} copy-done((f32[80,24,136]{0,2,1:T(8,128)S(1)}, f32[80,24,136]{0,2,1:T(8,128)}, u32[]{:S(2)}) %copy-start.3) | copy-done | bytes 1044504
  1.4 0.0 copy-start.7
  1.4 0.7 copy-done.7
  2.2 0.0 copy-start.8
  2.2 0.7 copy-done.8
  2.8 0.0 copy-start.9
  2.8 0.7 copy-done.9
  3.5 7.3 %pack.1 = f32[32,88,128]{2,1,0:T(8,128)} custom-call(s32[1]{0:T(128)} %bitcast.3.refs_0_, s32[24]{0:T(128)S(1)} %copy-done.9, s32[20,128]{1,0:T(8,128)S(1)} %bitcast.14, f32[1,80]{1,0:T(1,128)S(1)} %bitcast.15, f32[24,136,80]{2,1,0:T(8,128)S(1)} %bitcast.13), custom_call_target="tpu_custom_call" | custom-call | tf_op jit(solution)/shard_map/pack/pallas_call | solution.py:98
  10.8 12.0 %all-to-all-start = ((f32[32,88,128]{2,1,0:T(8,128)}), f32[32,88,128]{2,1,0:T(8,128)S(1)}, u32[]{:S(2)}, u32[]{:S(2)}) async-start(f32[32,88,128]{2,1,0:T(8,128)} %pack.1), calls=%async_computation | async-start | bytes 2883584 | tf_op jit(solution)/shard_map/all_to_all | solution.py:299
  22.8 0.0 copy-start.2
  22.8 2.9 %copy-done.2 = f32[1,2,640,1280]{3,2,1,0:T(8,128)S(1)} copy-done((f32[1,2,640,1280]{3,2,1,0:T(8,128)S(1)}, f32[1,2,640,1280]{3,2,1,0:T(8,128)}, u32[]{:S(2)}) %copy-start.2) | copy-done | bytes 6553624
  25.7 1.4 %split_table.1 = bf16[2,2,640,1280]{3,2,1,0:T(8,128)(2,1)S(1)} custom-call(f32[2,640,1280]{2,1,0:T(8,128)S(1)} %bitcast.12), custom_call_target="tpu_custom_call" | custom-call | tf_op jit(solution)/shard_map/split_table/pallas_call | solution.py:47
  27.1 0.0 copy-start
  27.1 2.7 %copy-done = bf16[2,2,640,1280]{3,2,1,0:T(8,128)(2,1)} copy-done((bf16[2,2,640,1280]{3,2,1,0:T(8,128)(2,1)}, bf16[2,2,640,1280]{3,2,1,0:T(8,128)(2,1)S(1)}, u32[]{:S(2)}) %copy-start) | copy-done | bytes 6553624
  29.8 27.1 %all-to-all-done.refs_0_ = f32[32,88,128]{2,1,0:T(8,128)S(1)} async-done(((f32[32,88,128]{2,1,0:T(8,128)}), f32[32,88,128]{2,1,0:T(8,128)S(1)}, u32[]{:S(2)}, u32[]{:S(2)}) %all-to-all-start) | async-done | bytes 1441824 | tf_op jit(solution)/shard_map/all_to_all | solution.py:299
  56.9 0.0 copy-start.1
  56.9 2.9 %copy-done.1 = bf16[2,2,640,1280]{3,2,1,0:T(8,128)(2,1)S(1)} copy-done((bf16[2,2,640,1280]{3,2,1,0:T(8,128)(2,1)S(1)}, bf16[2,2,640,1280]{3,2,1,0:T(8,128)(2,1)}, u32[]{:S(2)}) %copy-start.1) | copy-done | bytes 6553624
  59.8 6.4 %legendre_b.1 = f32[8,96,128]{2,1,0:T(8,128)S(1)} custom-call(f32[32,88,128]{2,1,0:T(8,128)S(1)} %all-to-all-done.refs_0_, bf16[2,1280,1280]{2,1,0:T(8,128)(2,1)S(1)} %bitcast.10), custom_call_target="tpu_custom_call" | custom-call | tf_op jit(solution)/shard_map/legendre_b/pallas_call | solution.py:205
  66.2 4.5 %legendre_a.1 = f32[8,80,128]{2,1,0:T(8,128)S(1)} custom-call(f32[32,88,128]{2,1,0:T(8,128)S(1)} %all-to-all-done.refs_0_, bf16[2,1280,1280]{2,1,0:T(8,128)(2,1)S(1)} %bitcast.11), custom_call_target="tpu_custom_call" | custom-call | tf_op jit(solution)/shard_map/legendre_a/pallas_call | solution.py:160
  70.7 0.0 copy-start.11
  70.7 0.0 copy-start.10
  70.7 0.0 copy-start.4
  70.7 0.0 copy-start.5
  70.7 0.0 copy-start.6
  70.8 0.9 pad_maximum_fusion
  71.7 7.9 %all-to-all-start.1 = ((f32[8,176,128]{2,1,0:T(8,128)}), f32[8,176,128]{2,1,0:T(8,128)S(1)}, u32[]{:S(2)}, u32[]{:S(2)}) async-start(f32[8,176,128]{2,1,0:T(8,128)} %pad_maximum_fusion), calls=%async_computation.1 | async-start | bytes 1441792 | tf_op jit(solution)/shard_map/all_to_all | solution.py:303
  79.6 0.0 copy-done.11
  79.6 0.1 copy.10.rates_ref
  79.7 0.0 copy-done.10
  79.7 0.7 fusion
  81.0 0.1 pad_add_fusion.base_ref
  81.1 10.0 %all-to-all-done.1.x_ref = f32[8,176,128]{2,1,0:T(8,128)S(1)} async-done(((f32[8,176,128]{2,1,0:T(8,128)}), f32[8,176,128]{2,1,0:T(8,128)S(1)}, u32[]{:S(2)}, u32[]{:S(2)}) %all-to-all-start.1) | async-done | bytes 720928 | tf_op jit(solution)/shard_map/all_to_all | solution.py:303
  91.0 0.0 copy-done.4
  91.0 0.0 copy-done.5
  91.0 0.0 copy-done.6
  91.1 2.9 %vertical.1 = f32[2,80,1088]{2,1,0:T(8,128)} custom-call(s32[2]{0:T(128)S(1)} %pad_add_fusion.base_ref, f32[136,136]{1,0:T(8,128)S(1)} %copy-done.4, f32[136,136]{1,0:T(8,128)S(1)} %copy-done.5, f32[136,136]{1,0:T(8,128)S(1)} %copy-done.6, f32[136,1]{1,0:T(8,128)S(1)} %copy.10.rates_ref, f32[8,176,128]{2,1,0:T(8,128)S(1)} %all-to-all-done.1.x_ref), custom_call_target="tpu_custom_call" | custom-call | tf_op jit(solution)/shard_map/vertical/pallas_call | solution.py:265
Async XLA Ops:
  0.0 1.4 %copy-start.3 = (f32[80,24,136]{0,2,1:T(8,128)S(1)}, f32[80,24,136]{0,2,1:T(8,128)}, u32[]{:S(2)}) copy-start(f32[80,24,136]{0,2,1:T(8,128)} %param.9) | copy-start | bytes 3133444
  1.4 0.7 copy-start.7
  2.2 0.7 copy-start.8
  2.8 0.7 copy-start.9
  10.8 46.1 %all-to-all-start = ((f32[32,88,128]{2,1,0:T(8,128)}), f32[32,88,128]{2,1,0:T(8,128)S(1)}, u32[]{:S(2)}, u32[]{:S(2)}) async-start(f32[32,88,128]{2,1,0:T(8,128)} %pack.1), calls=%async_computation | async-start | bytes 2883584 | tf_op jit(solution)/shard_map/all_to_all | solution.py:299
  22.8 2.9 %copy-start.2 = (f32[1,2,640,1280]{3,2,1,0:T(8,128)S(1)}, f32[1,2,640,1280]{3,2,1,0:T(8,128)}, u32[]{:S(2)}) copy-start(f32[1,2,640,1280]{3,2,1,0:T(8,128)} %param.13) | copy-start | bytes 19660804
  27.1 2.7 %copy-start = (bf16[2,2,640,1280]{3,2,1,0:T(8,128)(2,1)}, bf16[2,2,640,1280]{3,2,1,0:T(8,128)(2,1)S(1)}, u32[]{:S(2)}) copy-start(bf16[2,2,640,1280]{3,2,1,0:T(8,128)(2,1)S(1)} %split_table.1) | copy-start | bytes 19660804
  56.9 2.9 %copy-start.1 = (bf16[2,2,640,1280]{3,2,1,0:T(8,128)(2,1)S(1)}, bf16[2,2,640,1280]{3,2,1,0:T(8,128)(2,1)}, u32[]{:S(2)}) copy-start(bf16[2,2,640,1280]{3,2,1,0:T(8,128)(2,1)} %copy-done) | copy-start | bytes 19660804
  70.7 8.9 %copy-start.11 = (f32[136]{0:T(256)S(1)}, f32[136]{0:T(256)}, u32[]{:S(2)}) copy-start(f32[136]{0:T(256)} %param.16) | copy-start | bytes 1636
  70.7 9.0 %copy-start.10 = (s32[24]{0:T(128)S(1)}, s32[24]{0:T(128)}, u32[]{:S(2)}) copy-start(s32[24]{0:T(128)} %refs_1_.1) | copy-start | bytes 292
  70.7 20.3 %copy-start.4 = (f32[136,136]{1,0:T(8,128)S(1)}, f32[136,136]{1,0:T(8,128)}, u32[]{:S(2)}) copy-start(f32[136,136]{1,0:T(8,128)} %to_ref.1) | copy-start | bytes 221956
  70.7 20.3 %copy-start.5 = (f32[136,136]{1,0:T(8,128)S(1)}, f32[136,136]{1,0:T(8,128)}, u32[]{:S(2)}) copy-start(f32[136,136]{1,0:T(8,128)} %from_ref.1) | copy-start | bytes 221956
  70.7 20.3 %copy-start.6 = (f32[136,136]{1,0:T(8,128)S(1)}, f32[136,136]{1,0:T(8,128)}, u32[]{:S(2)}) copy-start(f32[136,136]{1,0:T(8,128)} %thermal_ref.1) | copy-start | bytes 221956
  71.7 19.4 %all-to-all-start.1 = ((f32[8,176,128]{2,1,0:T(8,128)}), f32[8,176,128]{2,1,0:T(8,128)S(1)}, u32[]{:S(2)}, u32[]{:S(2)}) async-start(f32[8,176,128]{2,1,0:T(8,128)} %pad_maximum_fusion), calls=%async_computation.1 | async-start | bytes 1441792 | tf_op jit(solution)/shard_map/all_to_all | solution.py:303

commit v2 on v1

v2 whole, which is shorter than its diff:
```python
import functools

import jax
import jax.numpy as jnp
from jax import lax
from jax.experimental import pallas as pl
from jax.experimental.pallas import tpu as pltpu
from jax.sharding import PartitionSpec as P

NTRUNC = 1280
LEVELS = 136
HALF = 64
F32 = jnp.float32
BF16 = jnp.bfloat16
VMEM = pltpu.VMEM


def whole():
    return pl.BlockSpec(memory_space=VMEM)


def smem():
    return pl.BlockSpec(memory_space=pltpu.SMEM)


def params(mb):
    return pltpu.CompilerParams(vmem_limit_bytes=mb << 20)


def lanes_of(shape):
    return lax.broadcasted_iota(jnp.int32, shape, 1)


def split(x):
    high = x.astype(BF16)
    low = (x - high.astype(F32)).astype(BF16)
    return high, low


def hbm():
    return pl.BlockSpec(memory_space=pltpu.HBM)


def stay(x):
    return pltpu.with_memory_space_constraint(x, pltpu.HBM)


def table_kernel(table_hbm, out_hbm, buf, halves, in_sem, out_sem):
    parities, _, rows, _ = out_hbm.shape
    step = buf.shape[1]
    parts = [(p, r) for p in range(parities) for r in range(0, rows, step)]
    reads = [
        pltpu.make_async_copy(table_hbm.at[p, r : r + step], buf.at[n], in_sem.at[n])
        for n, (p, r) in enumerate(parts)
    ]
    writes = [
        pltpu.make_async_copy(halves.at[n], out_hbm.at[p, :, r : r + step], out_sem.at[n])
        for n, (p, r) in enumerate(parts)
    ]
    for c in reads:
        c.start()
    for n, c in enumerate(reads):
        c.wait()
        high, low = split(buf[n])
        halves[n, 0] = high
        halves[n, 1] = low
        writes[n].start()
    for c in writes:
        c.wait()


def split_table(table):
    parities, rows, lats = table.shape
    n, step = parities * 4, rows // 4
    return pl.pallas_call(
        table_kernel,
        out_shape=pltpu.HBM((parities, 2, rows, lats), BF16),
        in_specs=[hbm()],
        out_specs=hbm(),
        scratch_shapes=[
            VMEM((n, step, lats), F32),
            VMEM((n, 2, step, lats), BF16),
            pltpu.SemaphoreType.DMA((n,)),
            pltpu.SemaphoreType.DMA((n,)),
        ],
        compiler_params=params(16),
        name="split_table",
    )(stay(table))


def load(refs):
    copies = [pltpu.make_async_copy(*r) for r in refs]
    for c in copies:
        c.start()
    for c in copies:
        c.wait()


def order_of(order, map_ref, slots):
    @pl.loop(0, slots)
    def _(s):
        order[s] = -1

    @pl.loop(0, map_ref.shape[0])
    def _(j):
        order[map_ref[j]] = j


def points_of(points, w, lat):
    first = w * lat
    row = first // 128
    off = first - row * 128
    lane = lanes_of((1, 128))
    back = lax.rem(128 - off, 128)
    here = pltpu.roll(points[pl.ds(row, 1), :], back, 1)
    after = pltpu.roll(points[pl.ds(jnp.minimum(row + 1, points.shape[0] - 1), 1), :], back, 1)
    return jnp.where(lane < 128 - off, here, after)[:, :lat]


def scaled(j, stride, points, weights, x):
    jj = jnp.maximum(j, 0)
    live = (2 * stride * jj < points) & (j >= 0)
    return x[jj] * jnp.where(live, weights, 0.0)


def two_up(x):
    y = jnp.transpose(x)
    half = y.shape[0] // 2
    return jnp.concatenate([y[:half], y[half:]], axis=1)


def pack_kernel(stride, where_ref, map_hbm, points_hbm, weights_hbm, x_hbm, out_ref, order, map_ref, pts, wts, x, sem):
    load(
        [
            (points_hbm, pts, sem.at[0]),
            (weights_hbm, wts, sem.at[1]),
            (map_hbm, map_ref, sem.at[2]),
            (x_hbm, x, sem.at[3]),
        ]
    )
    lat = x.shape[2]
    slots = out_ref.shape[0]
    order_of(order, map_ref, slots)
    points = points_of(pts, where_ref[0], lat)
    weights = wts[...]
    for s in range(slots):
        v = scaled(order[s], stride, points, weights, x)
        out_ref[s, 0:40, :] = two_up(v[:HALF])
        out_ref[s, 40:80, :] = two_up(v[HALF : 2 * HALF])
        out_ref[s, 80:88, :] = jnp.concatenate([v[2 * HALF :], jnp.zeros((8, 128 - lat), F32)], axis=1)


def pack(where, slot_map, points, weights, x, slots, stride):
    return pl.pallas_call(
        functools.partial(pack_kernel, stride),
        out_shape=jax.ShapeDtypeStruct((slots, 88, 128), F32),
        in_specs=[smem(), hbm(), hbm(), hbm(), hbm()],
        out_specs=whole(),
        scratch_shapes=[
            pltpu.SMEM((slots,), jnp.int32),
            pltpu.SMEM(slot_map.shape, jnp.int32),
            VMEM(points.shape, jnp.int32),
            VMEM(weights.shape, F32),
            VMEM(x.shape, F32),
            pltpu.SemaphoreType.DMA((4,)),
        ],
        compiler_params=params(8),
        name="pack",
    )(where, stay(slot_map), stay(points), stay(weights), stay(x))


def flip_rows(x):
    rows = lax.broadcasted_iota(jnp.int32, (8, 128), 0)
    tiles = [
        jnp.take_along_axis(x[8 * t : 8 * t + 8], 7 - rows, axis=0) for t in reversed(range(x.shape[0] // 8))
    ]
    return jnp.concatenate(tiles, axis=0)


def pair_main(north, south):
    other = pltpu.roll(flip_rows(south), HALF, 1)
    return north + other, north - other


def high_low(x):
    high = x.astype(BF16).astype(F32)
    return high, x - high


def store_main(dst, p, w, at, packed):
    high, low = high_low(packed)
    left = lanes_of(high.shape) < HALF
    dst[p, pl.ds(80 * w, 40), at : at + 128] = jnp.where(left, high, pltpu.roll(low, HALF, 1))
    dst[p, pl.ds(80 * w + 40, 40), at : at + 128] = jnp.where(left, pltpu.roll(high, HALF, 1), low)


def fold(t, shift):
    return t + pltpu.roll(t, 128 - shift, 1)


def products(table_ref, rhs, p):
    o = jnp.dot(table_ref[p], rhs[p].astype(BF16), preferred_element_type=F32)
    half = o.shape[0] // 2
    return o[:half] + o[half:]


def extra_columns(x_ref, rhs, half):
    zn = jnp.transpose(x_ref[0:half, 80:88, :].reshape(8 * half, 128))[:80]
    zs = flip_rows(jnp.transpose(x_ref[half:, 80:88, :].reshape(8 * half, 128))[:80])
    lane = lanes_of((8, 128))
    swap = 8 * (half - 1 - lane // 8) + lane % 8
    zs = jnp.concatenate([jnp.take_along_axis(zs[8 * t : 8 * t + 8], swap, axis=1) for t in range(10)], axis=0)
    even_group = (lanes_of((80, 128)) // 8) % 2 == 0
    for p, v in enumerate((zn + zs, zn - zs)):
        high, low = high_low(v)
        both = (
            jnp.where(even_group, high, pltpu.roll(low, 8, 1)),
            jnp.where(even_group, pltpu.roll(high, 120, 1), low),
        )
        for w in range(half):
            rhs[p, 80 * w : 80 * w + 80, 256:384] = pltpu.roll(both[w % 2], (128 - 16 * (w // 2)) % 128, 1)


def legendre_kernel(x_ref, table_hbm, out_ref, rhs, table, sem):
    reads = [pltpu.make_async_copy(table_hbm.at[p], table.at[p], sem.at[p]) for p in range(2)]
    for c in reads:
        c.start()
    blocks = x_ref.shape[0]
    half = blocks // 2
    members = out_ref.shape[0]
    extra_columns(x_ref, rhs, half)

    @pl.loop(0, half, unroll=4)
    def _(w):
        for at in (0, 40):
            north, south = x_ref[w, at : at + 40, :], x_ref[blocks - 1 - w, at : at + 40, :]
            for p, v in enumerate(pair_main(north, south)):
                store_main(rhs, p, w, 128 * (at // 40), v)

    reads[0].wait()
    even = products(table, rhs, 0)
    reads[1].wait()
    odd = products(table, rhs, 1)
    for n in range(2):
        e, o = fold(even[:, 128 * n : 128 * n + 128], HALF), fold(odd[:, 128 * n : 128 * n + 128], HALF)
        res = jnp.where(lanes_of(e.shape) < HALF, e, o)
        out_ref[:, 80 * n : 80 * n + 80, :] = res.reshape(members, 80, 128)
    ee, oo = fold(even[:, 256:], 8), fold(odd[:, 256:], 8)
    extra = jnp.where(lanes_of(ee.shape) < 8, ee, pltpu.roll(oo, 8, 1)).reshape(members, 80, 128)
    for k in range(members):
        padded = jnp.concatenate([extra[k], jnp.zeros((48, 128), F32)], axis=0)
        out_ref[k, 160:176, :] = jnp.transpose(padded)[:16]


def legendre(x, table, members):
    rows = table.shape[1] // 2
    return pl.pallas_call(
        legendre_kernel,
        out_shape=jax.ShapeDtypeStruct((members, 2 * rows // members + 16, 128), F32),
        in_specs=[whole(), hbm()],
        out_specs=whole(),
        scratch_shapes=[
            VMEM((2, table.shape[2], 384), F32),
            VMEM(table.shape, BF16),
            pltpu.SemaphoreType.DMA((2,)),
        ],
        compiler_params=params(20),
        name="legendre",
    )(x, stay(table))


def dot3(a, b):
    ah, al = split(a)
    bh, bl = split(b)
    d = lambda u, v: jnp.dot(u, v, preferred_element_type=F32)
    return d(ah, bh) + (d(ah, bl) + d(al, bh))


def vertical_kernel(stride, where_ref, map_ref, to_ref, from_ref, thermal_ref, rates_ref, *refs):
    x_ref, out_ref, y = refs
    members = x_ref.shape[0]
    here = where_ref[0]
    me = where_ref[1]
    row0 = 80 * me
    base = lax.fori_loop(
        0, map_ref.shape[0], lambda j, b: jnp.where(map_ref[j] == here, stride * j, b), jnp.int32(0)
    )
    lane = lanes_of((1, 128))
    degree = [base + 2 * (row0 + lane) + p for p in range(2)]
    live = [(d < NTRUNC) & (lane < 80) for d in degree]
    pad = jnp.zeros((48, 128), F32)
    for l in range(members):
        for n in range(2):
            t = jnp.transpose(jnp.concatenate([x_ref[l, 80 * n : 80 * n + 80], pad], axis=0))
            for p in range(2):
                at = 136 * l + 64 * n
                y[p, at : at + 64, :] = jnp.where(live[p], t[64 * p : 64 * p + 64], 0.0)
        for p in range(2):
            v = x_ref[l, 160 + 8 * p : 168 + 8 * p]
            y[p, 136 * l + 128 : 136 * l + 136, :] = jnp.where(live[p], v, 0.0)
    div = jnp.concatenate(
        [y[p, pl.ds(2 + part, LEVELS, stride=8), :] for p in range(2) for part in range(2)], axis=1
    )
    modal = dot3(to_ref[...], div)
    damp = []
    for p in range(2):
        d = degree[p].astype(F32)
        ratio = d * (d + 1.0) / (NTRUNC * NTRUNC)
        damp.append(1.0 / (1.0 + rates_ref[...] * ratio))
    damped = modal * jnp.concatenate([damp[0], damp[0], damp[1], damp[1]], axis=1)
    new = dot3(from_ref[...], damped)
    heat = dot3(thermal_ref[...], new)
    for p in range(2):
        for part in range(2):
            at = 128 * (2 * p + part)
            y[p, pl.ds(2 + part, LEVELS, stride=8), :] = new[:, at : at + 128]
            t = y[p, pl.ds(4 + part, LEVELS, stride=8), :]
            y[p, pl.ds(4 + part, LEVELS, stride=8), :] = t - heat[:, at : at + 128]
    for p in range(2):
        for c in range(8):
            out_ref[p, :, 128 * c : 128 * c + 128] = jnp.transpose(y[p, 128 * c : 128 * c + 128, :])[:80]
        tail = jnp.concatenate([y[p, 1024:1088, :], jnp.zeros((64, 128), F32)], axis=0)
        out_ref[p, :, 1024:1088] = jnp.transpose(tail)[:80, :64]


def vertical(where, slot_map, to_modes, from_modes, thermal, rates, x, stride):
    return pl.pallas_call(
        lambda *refs: vertical_kernel(stride, *refs),
        out_shape=jax.ShapeDtypeStruct((2, 80, 8 * LEVELS), F32),
        in_specs=[smem(), smem()] + [whole()] * 5,
        out_specs=whole(),
        scratch_shapes=[VMEM((2, 8 * LEVELS, 128), F32)],
        compiler_params=params(12),
        name="vertical",
    )(where, slot_map, to_modes, from_modes, thermal, rates, x)


def on_device(
    fourier,
    weights,
    row_points,
    slot_map,
    legendre_lookup,
    to_modes,
    from_modes,
    mode_rates,
    thermal_response_matrix,
):
    members = lax.axis_size("lev")
    w = lax.axis_index("wave")
    l = lax.axis_index("lev")
    lat, window, _ = fourier.shape
    stride = NTRUNC // window
    where = jnp.stack([w, l]).astype(jnp.int32)
    x = jnp.transpose(fourier, (1, 2, 0))
    points = row_points.reshape(-1, 128)
    wts = weights.reshape(1, lat)
    sent = pack(where, slot_map, points, wts, x, lax.axis_size("wave"), stride)
    arrived = lax.all_to_all(sent, "wave", split_axis=0, concat_axis=0, tiled=True)
    table = split_table(legendre_lookup[0]).reshape(2, 1280, 1280)
    local = legendre(arrived, table, members)
    mine = lax.all_to_all(local, "lev", split_axis=0, concat_axis=0, tiled=True)
    rates = mode_rates.reshape(-1, 1)
    out = vertical(where, slot_map, to_modes, from_modes, thermal_response_matrix, rates, mine, stride)
    return out[None]


def solution(mesh):
    placed = (
        P("wave", None, "lev"),
        P("wave"),
        P(),
        P(),
        P("wave", None, None, None),
        P(),
        P(),
        P(),
        P(),
    )
    return jax.shard_map(
        on_device,
        mesh=mesh,
        in_specs=placed,
        out_specs=P("wave", None, "lev", None),
        check_vma=False,
    )
```

time: 94.4 us -> 80.7 us (0.85)
  local copies, waits for them, and re-layouts: 12 us -> 0.12 us
  waiting for transfers between devices: 37 us -> 39.7 us
  Pallas kernels: 22.6 us -> 20.5 us
  other arithmetic: 1.65 us -> 0.07 us
    unnamed x24 -> x10, local copies, waits for them, and re-layouts: 11.9 us -> 0.02 us
    pallas_call x5 -> x4, Pallas kernels: 22.6 us -> 20.5 us  [the longest x1 7.33 us: legendre(): pl.pallas_call(legendre_kernel, out_shape=jax.ShapeDtypeStruct((members,...]
    all_to_all x1, waiting for transfers between devices: 9.95 us -> 11.3 us  [on_device(): mine = lax.all_to_all(local, 'lev', split_axis=0, concat_axis=0, tiled=True)]
    all_to_all x1, waiting for transfers between devices: 27.1 us -> 28.3 us  [on_device(): lax.all_to_all(sent, 'wave', split_axis=0, concat_axis=0, tiled=True)]
  transfers between devices with their start and end apart: 2 -> 2, of which waited for: 2 -> 2; matrix products, arithmetic and copies ran while one was open for 1% -> 0% of each run, Pallas kernels for 1% -> 7%
where the time goes in v2:
time: 80.7 us; the launch traced here: 80.4 us
  waiting for transfers between devices  39.7 us (49%)
  Pallas kernels  20.5 us (25%)
  starting transfers between devices  20 us (25%)
    all_to_all x1, waiting for transfers between devices, on_device(): lax.all_to_all(sent, 'wave', split_axis=0, concat_axis=0, tiled=True)  28.3 us
    all_to_all x1, starting transfers between devices, on_device(): lax.all_to_all(sent, 'wave', split_axis=0, concat_axis=0, tiled=True)  12 us
    all_to_all x1, waiting for transfers between devices, on_device(): mine = lax.all_to_all(local, 'lev', split_axis=0, concat_axis=0, tiled=True)  11.3 us
    all_to_all x1, starting transfers between devices, on_device(): mine = lax.all_to_all(local, 'lev', split_axis=0, concat_axis=0, tiled=True)  7.93 us
    pallas_call x1, Pallas kernels, legendre(): pl.pallas_call(legendre_kernel, out_shape=jax.ShapeDtypeStruct((members,...  7.33 us
    pallas_call x1, Pallas kernels, split_table(): pl.pallas_call(table_kernel, out_shape=pltpu.HBM((parities, 2, rows, lats...  5.73 us
    pallas_call x1, Pallas kernels, pack(): pl.pallas_call(functools.partial(pack_kernel, stride), out_shape=jax.Shap...  4.39 us
    pallas_call x1, Pallas kernels, vertical(): pl.pallas_call(lambda *refs: vertical_kernel(stride, *refs), out_shape=ja...  3.04 us
  transfers between devices with their start and end apart: 2, of which 2 were waited for; matrix products, arithmetic and copies ran while one was open for 0% of the time, Pallas kernels for 7%

profile of v2, /device:TPU:1, one launch (start us, length us, event | category | flops | bytes accessed | tf_op | source)
XLA Modules:
  0.0 80.4 jit_solution(16516183087763091744)
XLA Ops:
  0.0 0.1 pad_add_fusion.where_ref.refs_0_
  0.1 4.4 %pack.1 = f32[32,88,128]{2,1,0:T(8,128)} custom-call(s32[2]{0:T(128)S(1)} %pad_add_fusion.where_ref.refs_0_, s32[24]{0:T(128)} %refs_1_.1, s32[20,128]{1,0:T(8,128)} %bitcast.12, f32[1,80]{1,0:T(1,128)} %bitcast.14, f32[24,136,80]{2,1,0:T(8,128)} %bitcast.11), custom_call_target="tpu_custom_call" | custom-call | tf_op jit(solution)/shard_map/pack/pallas_call | solution.py:154
  4.5 12.0 %all-to-all-start = ((f32[32,88,128]{2,1,0:T(8,128)}), f32[32,88,128]{2,1,0:T(8,128)S(1)}, u32[]{:S(2)}, u32[]{:S(2)}) async-start(f32[32,88,128]{2,1,0:T(8,128)} %pack.1), calls=%async_computation | async-start | bytes 2883584 | tf_op jit(solution)/shard_map/all_to_all | solution.py:359
  16.5 5.7 %split_table.1 = bf16[2,2,640,1280]{3,2,1,0:T(8,128)(2,1)} custom-call(f32[2,640,1280]{2,1,0:T(8,128)} %bitcast.10), custom_call_target="tpu_custom_call" | custom-call | tf_op jit(solution)/shard_map/split_table/pallas_call | solution.py:75
  22.3 28.3 %all-to-all-done.x_ref = f32[32,88,128]{2,1,0:T(8,128)S(1)} async-done(((f32[32,88,128]{2,1,0:T(8,128)}), f32[32,88,128]{2,1,0:T(8,128)S(1)}, u32[]{:S(2)}, u32[]{:S(2)}) %all-to-all-start) | async-done | bytes 1441824 | tf_op jit(solution)/shard_map/all_to_all | solution.py:359
  50.6 0.0 copy-start.4
  50.6 0.0 copy-start
  50.6 0.0 copy-start.1
  50.6 0.0 copy-start.2
  50.6 0.0 copy-start.3
  50.6 7.3 %legendre.1 = f32[8,176,128]{2,1,0:T(8,128)} custom-call(f32[32,88,128]{2,1,0:T(8,128)S(1)} %all-to-all-done.x_ref, bf16[2,1280,1280]{2,1,0:T(8,128)(2,1)} %bitcast.9), custom_call_target="tpu_custom_call" | custom-call | tf_op jit(solution)/shard_map/legendre/pallas_call | solution.py:257
  57.9 7.9 %all-to-all-start.1 = ((f32[8,176,128]{2,1,0:T(8,128)}), f32[8,176,128]{2,1,0:T(8,128)S(1)}, u32[]{:S(2)}, u32[]{:S(2)}) async-start(f32[8,176,128]{2,1,0:T(8,128)} %legendre.1), calls=%async_computation.1 | async-start | bytes 1441792 | tf_op jit(solution)/shard_map/all_to_all | solution.py:362
  65.9 0.0 copy-done.4
  65.9 0.1 copy.10.refs_5_
  66.0 11.3 %all-to-all-done.1.refs_6_ = f32[8,176,128]{2,1,0:T(8,128)S(1)} async-done(((f32[8,176,128]{2,1,0:T(8,128)}), f32[8,176,128]{2,1,0:T(8,128)S(1)}, u32[]{:S(2)}, u32[]{:S(2)}) %all-to-all-start.1) | async-done | bytes 720928 | tf_op jit(solution)/shard_map/all_to_all | solution.py:362
  77.3 0.0 copy-done
  77.3 0.0 copy-done.1
  77.3 0.0 copy-done.2
  77.3 0.0 copy-done.3
  77.4 3.0 %vertical.1 = f32[2,80,1088]{2,1,0:T(8,128)} custom-call(s32[2]{0:T(128)S(1)} %pad_add_fusion.where_ref.refs_0_, s32[24]{0:T(128)S(1)} %copy-done.3, f32[136,136]{1,0:T(8,128)S(1)} %copy-done, f32[136,136]{1,0:T(8,128)S(1)} %copy-done.1, f32[136,136]{1,0:T(8,128)S(1)} %copy-done.2, f32[136,1]{1,0:T(8,128)S(1)} %copy.10.refs_5_, ...), custom_call_target="tpu_custom_call" | custom-call | tf_op jit(solution)/shard_map/vertical/pallas_call | solution.py:327
Async XLA Ops:
  4.5 46.1 %all-to-all-start = ((f32[32,88,128]{2,1,0:T(8,128)}), f32[32,88,128]{2,1,0:T(8,128)S(1)}, u32[]{:S(2)}, u32[]{:S(2)}) async-start(f32[32,88,128]{2,1,0:T(8,128)} %pack.1), calls=%async_computation | async-start | bytes 2883584 | tf_op jit(solution)/shard_map/all_to_all | solution.py:359
  50.6 15.3 %copy-start.4 = (f32[136]{0:T(256)S(1)}, f32[136]{0:T(256)}, u32[]{:S(2)}) copy-start(f32[136]{0:T(256)} %param.16) | copy-start | bytes 1636
  50.6 26.7 %copy-start = (f32[136,136]{1,0:T(8,128)S(1)}, f32[136,136]{1,0:T(8,128)}, u32[]{:S(2)}) copy-start(f32[136,136]{1,0:T(8,128)} %refs_2_.1) | copy-start | bytes 221956
  50.6 26.7 %copy-start.1 = (f32[136,136]{1,0:T(8,128)S(1)}, f32[136,136]{1,0:T(8,128)}, u32[]{:S(2)}) copy-start(f32[136,136]{1,0:T(8,128)} %refs_3_.1) | copy-start | bytes 221956
  50.6 26.7 %copy-start.2 = (f32[136,136]{1,0:T(8,128)S(1)}, f32[136,136]{1,0:T(8,128)}, u32[]{:S(2)}) copy-start(f32[136,136]{1,0:T(8,128)} %refs_4_.1) | copy-start | bytes 221956
  50.6 26.7 %copy-start.3 = (s32[24]{0:T(128)S(1)}, s32[24]{0:T(128)}, u32[]{:S(2)}) copy-start(s32[24]{0:T(128)} %refs_1_.1) | copy-start | bytes 292
  57.9 19.4 %all-to-all-start.1 = ((f32[8,176,128]{2,1,0:T(8,128)}), f32[8,176,128]{2,1,0:T(8,128)S(1)}, u32[]{:S(2)}, u32[]{:S(2)}) async-start(f32[8,176,128]{2,1,0:T(8,128)} %legendre.1), calls=%async_computation.1 | async-start | bytes 1441792 | tf_op jit(solution)/shard_map/all_to_all | solution.py:362

commit v3 on v2

v3 whole, which is shorter than its diff:
```python
import functools

import jax
import jax.numpy as jnp
from jax import lax
from jax.experimental import pallas as pl
from jax.experimental.pallas import tpu as pltpu
from jax.sharding import PartitionSpec as P


NTRUNC = 1280
LEVELS = 136
F32 = jnp.float32
BF16 = jnp.bfloat16
VMEM = pltpu.VMEM


def whole():
    return pl.BlockSpec(memory_space=VMEM)


def smem():
    return pl.BlockSpec(memory_space=pltpu.SMEM)


def params(mb):
    return pltpu.CompilerParams(vmem_limit_bytes=mb << 20)


def lanes_of(shape):
    return lax.broadcasted_iota(jnp.int32, shape, 1)


def split(x):
    high = x.astype(BF16)
    low = (x - high.astype(F32)).astype(BF16)
    return high, low


def hbm():
    return pl.BlockSpec(memory_space=pltpu.HBM)


def stay(x):
    return pltpu.with_memory_space_constraint(x, pltpu.HBM)


def table_kernel(table_hbm, out_hbm, buf, halves, in_sem, out_sem):
    parities, _, rows, _ = out_hbm.shape
    step = buf.shape[1]
    parts = [(p, r) for p in range(parities) for r in range(0, rows, step)]
    reads = [
        pltpu.make_async_copy(table_hbm.at[p, r : r + step], buf.at[n], in_sem.at[n])
        for n, (p, r) in enumerate(parts)
    ]
    writes = [
        pltpu.make_async_copy(halves.at[n], out_hbm.at[p, :, r : r + step], out_sem.at[n])
        for n, (p, r) in enumerate(parts)
    ]
    for c in reads:
        c.start()
    for n, c in enumerate(reads):
        c.wait()
        high, low = split(buf[n])
        halves[n, 0] = high
        halves[n, 1] = low
        writes[n].start()
    for c in writes:
        c.wait()


def split_table(table):
    parities, rows, lats = table.shape
    n, step = parities * 4, rows // 4
    return pl.pallas_call(
        table_kernel,
        out_shape=pltpu.HBM((parities, 2, rows, lats), BF16),
        in_specs=[hbm()],
        out_specs=hbm(),
        scratch_shapes=[
            VMEM((n, step, lats), F32),
            VMEM((n, 2, step, lats), BF16),
            pltpu.SemaphoreType.DMA((n,)),
            pltpu.SemaphoreType.DMA((n,)),
        ],
        compiler_params=params(16),
        name="split_table",
    )(stay(table))


def points_of(points, w, lat):
    first = w * lat
    row = first // 128
    off = first - row * 128
    lane = lanes_of((1, 128))
    back = lax.rem(128 - off, 128)
    here = pltpu.roll(points[pl.ds(row, 1), :], back, 1)
    after = pltpu.roll(points[pl.ds(jnp.minimum(row + 1, points.shape[0] - 1), 1), :], back, 1)
    return jnp.where(lane < 128 - off, here, after)[:, :lat]


def pack_kernel(stride, where_ref, map_hbm, points_hbm, weights_hbm, x_hbm, out_ref, filled, map_ref, pts, wts, x, sem):
    window = x.shape[0]
    chunks = sem.shape[0] - 3
    size = window // chunks

    def read(c):
        js = pl.ds(c * size, size)
        return pltpu.make_async_copy(x_hbm.at[js], x.at[js], sem.at[3 + c])

    small = [
        pltpu.make_async_copy(map_hbm, map_ref, sem.at[0]),
        pltpu.make_async_copy(points_hbm, pts, sem.at[1]),
        pltpu.make_async_copy(weights_hbm, wts, sem.at[2]),
    ]
    for c in small:
        c.start()
    for c in range(chunks):
        read(c).start()
    for c in small:
        c.wait()
    lat = x.shape[2]
    slots = out_ref.shape[0]

    @pl.loop(0, slots)
    def _(s):
        filled[s] = 0

    @pl.loop(0, window)
    def _(j):
        filled[map_ref[j]] = 1

    @pl.loop(0, slots)
    def _(s):
        @pl.when(filled[s] == 0)
        def _():
            out_ref[s] = jnp.zeros(out_ref.shape[1:], F32)

    points = points_of(pts, where_ref[0], lat)
    weights = wts[...]

    @pl.loop(0, chunks)
    def _(c):
        read(c).wait()
        for n in range(size):
            j = c * size + n
            s = map_ref[j]
            v = x[j] * jnp.where(2 * stride * j < points, weights, 0.0)
            out_ref[s, 0:80, :] = jnp.transpose(v[:128])
            out_ref[s, 80:88, :] = jnp.concatenate([v[128:], jnp.zeros((8, 128 - lat), F32)], axis=1)


def pack(where, slot_map, points, weights, x, slots, stride):
    return pl.pallas_call(
        functools.partial(pack_kernel, stride),
        out_shape=jax.ShapeDtypeStruct((slots, 88, 128), F32),
        in_specs=[smem(), hbm(), hbm(), hbm(), hbm()],
        out_specs=whole(),
        scratch_shapes=[
            pltpu.SMEM((slots,), jnp.int32),
            pltpu.SMEM(slot_map.shape, jnp.int32),
            VMEM(points.shape, jnp.int32),
            VMEM(weights.shape, F32),
            VMEM(x.shape, F32),
            pltpu.SemaphoreType.DMA((3 + 4,)),
        ],
        compiler_params=params(8),
        name="pack",
    )(where, stay(slot_map), stay(points), stay(weights), stay(x))


def flip_rows(x):
    rows = lax.broadcasted_iota(jnp.int32, (8, 128), 0)
    tiles = [
        jnp.take_along_axis(x[8 * t : 8 * t + 8], 7 - rows, axis=0) for t in reversed(range(x.shape[0] // 8))
    ]
    return jnp.concatenate(tiles, axis=0)


STEPS, AHEAD = 2, 2


def pairs(north, south):
    return north + south, north - south


def put(rhs, p, w, at, x):
    rows = pl.ds(80 * w, 80)
    high, low = split(x)
    rhs[p, 0, rows, at : at + 128] = high
    rhs[p, 1, rows, at : at + 128] = low


def extra_columns(x_ref, rhs, half):
    zn = jnp.transpose(x_ref[0:half, 80:88, :].reshape(8 * half, 128))[:80]
    zs = flip_rows(jnp.transpose(x_ref[half:, 80:88, :].reshape(8 * half, 128))[:80])
    lane = lanes_of((8, 128))
    swap = 8 * (half - 1 - lane // 8) + lane % 8
    zs = jnp.concatenate([jnp.take_along_axis(zs[8 * t : 8 * t + 8], swap, axis=1) for t in range(10)], axis=0)
    for p, v in enumerate(pairs(zn, zs)):
        for w in range(half):
            put(rhs, p, w, 128, pltpu.roll(v, (128 - 8 * w) % 128, 1))


def legendre_kernel(where_ref, x_ref, table_hbm, *refs):
    outs, (rhs, table, res, sem) = refs[:-4], refs[-4:]
    step = table.shape[2]
    count = table.shape[0]
    each = count // 2

    def read(n):
        p = n // each
        at = pl.multiple_of((n - p * each) * step, 8)
        return pltpu.make_async_copy(table_hbm.at[p, :, pl.ds(at, step)], table.at[n], sem.at[n])

    for n in range(AHEAD):
        read(n).start()
    blocks = x_ref.shape[0]
    half = blocks // 2
    me = where_ref[1]
    extra_columns(x_ref, rhs, half)

    @pl.loop(0, half, unroll=4)
    def _(w):
        for p, v in enumerate(pairs(x_ref[w, 0:80, :], flip_rows(x_ref[blocks - 1 - w, 0:80, :]))):
            put(rhs, p, w, 0, v)

    @pl.loop(0, count)
    def _(n):
        @pl.when(n + AHEAD < count)
        def _():
            read(n + AHEAD).start()

        read(n).wait()
        p = n // each
        at = pl.multiple_of((n - p * each) * step, 8)
        both = table[n].reshape(2 * step, table.shape[3])
        o = jnp.dot(both, rhs[p, 0], preferred_element_type=F32)
        q = jnp.dot(both[:step], rhs[p, 1], preferred_element_type=F32)
        res[p, pl.ds(at, step), :] = o[:step] + o[step:] + q

    for r, out in enumerate(outs):
        mine = pl.ds(pl.multiple_of(80 * (me ^ r), 8), 80)
        out[0:80, :] = res[0, mine, 0:128]
        out[80:160, :] = res[1, mine, 0:128]
        first, second = res[0, mine, 128:256], pltpu.roll(res[1, mine, 128:256], 8, 1)
        extra = jnp.where(lanes_of(first.shape) < 8, first, second)
        out[160:176, :] = jnp.transpose(jnp.concatenate([extra, jnp.zeros((48, 128), F32)], axis=0))[:16]


def legendre(where, x, table, members):
    parities, _, rows, lats = table.shape
    step = rows // STEPS
    piece = jax.ShapeDtypeStruct((2 * rows // members + 16, 128), F32)
    return pl.pallas_call(
        legendre_kernel,
        out_shape=[piece] * members,
        in_specs=[smem(), whole(), hbm()],
        out_specs=[whole()] * members,
        scratch_shapes=[
            VMEM((2, 2, lats, 256), BF16),
            VMEM((parities * STEPS, 2, step, lats), BF16),
            VMEM((2, rows, 256), F32),
            pltpu.SemaphoreType.DMA((parities * STEPS,)),
        ],
        compiler_params=params(24),
        name="legendre",
    )(where, x, stay(table))


def dot3(a, b):
    ah, al = split(a)
    bh, bl = split(b)
    d = lambda u, v: jnp.dot(u, v, preferred_element_type=F32)
    return d(ah, bh) + (d(ah, bl) + d(al, bh))


def vertical_kernel(stride, where_ref, map_ref, to_ref, from_ref, thermal_ref, rates_ref, *refs):
    pieces, (out_ref, y) = refs[:-2], refs[-2:]
    here = where_ref[0]
    me = where_ref[1]
    row0 = 80 * me
    base = lax.fori_loop(
        0, map_ref.shape[0], lambda j, b: jnp.where(map_ref[j] == here, stride * j, b), jnp.int32(0)
    )
    lane = lanes_of((1, 128))
    degree = [base + 2 * (row0 + lane) + p for p in range(2)]
    live = [(d < NTRUNC) & (lane < 80) for d in degree]
    pad = jnp.zeros((48, 128), F32)
    for r, x in enumerate(pieces):
        at = pl.multiple_of(136 * (me ^ r), 8)
        for p in range(2):
            t = jnp.transpose(jnp.concatenate([x[80 * p : 80 * p + 80], pad], axis=0))
            y[p, pl.ds(at, 128), :] = jnp.where(live[p], t, 0.0)
            y[p, pl.ds(at + 128, 8), :] = jnp.where(live[p], x[160 + 8 * p : 168 + 8 * p], 0.0)
    div = jnp.concatenate(
        [y[p, pl.ds(2 + part, LEVELS, stride=8), :] for p in range(2) for part in range(2)], axis=1
    )
    modal = dot3(to_ref[...], div)
    damp = []
    for p in range(2):
        d = degree[p].astype(F32)
        ratio = d * (d + 1.0) / (NTRUNC * NTRUNC)
        damp.append(1.0 / (1.0 + rates_ref[...] * ratio))
    damped = modal * jnp.concatenate([damp[0], damp[0], damp[1], damp[1]], axis=1)
    new = dot3(from_ref[...], damped)
    heat = dot3(thermal_ref[...], new)
    for p in range(2):
        for part in range(2):
            at = 128 * (2 * p + part)
            y[p, pl.ds(2 + part, LEVELS, stride=8), :] = new[:, at : at + 128]
            t = y[p, pl.ds(4 + part, LEVELS, stride=8), :]
            y[p, pl.ds(4 + part, LEVELS, stride=8), :] = t - heat[:, at : at + 128]
    for p in range(2):
        for c in range(8):
            out_ref[p, :, 128 * c : 128 * c + 128] = jnp.transpose(y[p, 128 * c : 128 * c + 128, :])[:80]
        tail = jnp.concatenate([y[p, 1024:1088, :], jnp.zeros((64, 128), F32)], axis=0)
        out_ref[p, :, 1024:1088] = jnp.transpose(tail)[:80, :64]


def vertical(where, slot_map, to_modes, from_modes, thermal, rates, pieces, stride):
    return pl.pallas_call(
        lambda *refs: vertical_kernel(stride, *refs),
        out_shape=jax.ShapeDtypeStruct((2, 80, 8 * LEVELS), F32),
        in_specs=[smem(), smem()] + [whole()] * (4 + len(pieces)),
        out_specs=whole(),
        scratch_shapes=[VMEM((2, 8 * LEVELS, 128), F32)],
        compiler_params=params(12),
        name="vertical",
    )(where, slot_map, to_modes, from_modes, thermal, rates, *pieces)


def on_device(
    fourier,
    weights,
    row_points,
    slot_map,
    legendre_lookup,
    to_modes,
    from_modes,
    mode_rates,
    thermal_response_matrix,
):
    members = lax.axis_size("lev")
    w = lax.axis_index("wave")
    l = lax.axis_index("lev")
    lat, window, _ = fourier.shape
    stride = NTRUNC // window
    where = jnp.stack([w, l]).astype(jnp.int32)
    x = jnp.transpose(fourier, (1, 2, 0))
    points = row_points.reshape(-1, 128)
    wts = weights.reshape(1, lat)
    sent = pack(where, slot_map, points, wts, x, lax.axis_size("wave"), stride)
    arrived = lax.all_to_all(sent, "wave", split_axis=0, concat_axis=0, tiled=True)
    table = split_table(legendre_lookup[0])
    local = legendre(where, arrived, table, members)
    mine = [local[0]]
    for r in range(1, members):
        mine.append(lax.ppermute(local[r], "lev", [(i, i ^ r) for i in range(members)]))
    rates = mode_rates.reshape(-1, 1)
    out = vertical(where, slot_map, to_modes, from_modes, thermal_response_matrix, rates, mine, stride)
    return out[None]


def solution(mesh):
    placed = (
        P("wave", None, "lev"),
        P("wave"),
        P(),
        P(),
        P("wave", None, None, None),
        P(),
        P(),
        P(),
        P(),
    )
    return jax.shard_map(
        on_device,
        mesh=mesh,
        in_specs=placed,
        out_specs=P("wave", None, "lev", None),
        check_vma=False,
    )
```

time: 80.7 us -> 78.6 us (0.974)
  starting transfers between devices: 20 us -> 23.7 us
  waiting for transfers between devices: 39.7 us -> 36.2 us
  Pallas kernels: 20.5 us -> 18.3 us
    ppermute x0 -> x7, starting transfers between devices: none -> 11.7 us  [on_device(): lax.ppermute(local[r], 'lev', [(i, i ^ r) for i in range(members)])]
    all_to_all x1 -> x0, waiting for transfers between devices: 11.3 us -> none  [on_device(): mine = lax.all_to_all(local, 'lev', split_axis=0, concat_axis=0, tiled=True)]
    all_to_all x1 -> x0, starting transfers between devices: 7.93 us -> none  [on_device(): mine = lax.all_to_all(local, 'lev', split_axis=0, concat_axis=0, tiled=True)]
    ppermute x0 -> x7, waiting for transfers between devices: none -> 7.92 us  [on_device(): lax.ppermute(local[r], 'lev', [(i, i ^ r) for i in range(members)])]
    pallas_call x1, Pallas kernels: 7.33 us -> 5.54 us  [legendre(): pl.pallas_call(legendre_kernel, out_shape=[piece] * members, in_specs=[sm...]
  transfers between devices with their start and end apart: 2 -> 8, of which waited for: 2 -> 5; matrix products, arithmetic and copies ran while one was open for 0% -> 0% of each run, Pallas kernels for 7% -> 7%
where the time goes in v3:
time: 78.6 us; the launch traced here: 78.5 us
  waiting for transfers between devices  36.2 us (46%)
  starting transfers between devices  23.7 us (30%)
  Pallas kernels  18.3 us (23%)
    all_to_all x1, waiting for transfers between devices, on_device(): lax.all_to_all(sent, 'wave', split_axis=0, concat_axis=0, tiled=True)  28.3 us
    all_to_all x1, starting transfers between devices, on_device(): lax.all_to_all(sent, 'wave', split_axis=0, concat_axis=0, tiled=True)  12 us
    ppermute x7, starting transfers between devices, on_device(): lax.ppermute(local[r], 'lev', [(i, i ^ r) for i in range(members)])  11.7 us
    ppermute x7, waiting for transfers between devices, on_device(): lax.ppermute(local[r], 'lev', [(i, i ^ r) for i in range(members)])  7.92 us
    pallas_call x1, Pallas kernels, split_table(): pl.pallas_call(table_kernel, out_shape=pltpu.HBM((parities, 2, rows, lats...  5.71 us
    pallas_call x1, Pallas kernels, legendre(): pl.pallas_call(legendre_kernel, out_shape=[piece] * members, in_specs=[sm...  5.54 us
    pallas_call x1, Pallas kernels, pack(): pl.pallas_call(functools.partial(pack_kernel, stride), out_shape=jax.Shap...  3.9 us
    pallas_call x1, Pallas kernels, vertical(): pl.pallas_call(lambda *refs: vertical_kernel(stride, *refs), out_shape=ja...  3.1 us
  transfers between devices with their start and end apart: 8, of which 5 were waited for; matrix products, arithmetic and copies ran while one was open for 0% of the time, Pallas kernels for 7%

profile of v3, /device:TPU:1, one launch (start us, length us, event | category | flops | bytes accessed | tf_op | source)
XLA Modules:
  0.0 78.5 jit_solution(13985090846669480011)
XLA Ops:
  0.0 0.1 pad_add_fusion.where_ref.refs_0_
  0.1 3.9 %pack.1 = f32[32,88,128]{2,1,0:T(8,128)} custom-call(s32[2]{0:T(128)S(1)} %pad_add_fusion.where_ref.refs_0_, s32[24]{0:T(128)} %refs_1_.1, s32[20,128]{1,0:T(8,128)} %bitcast.10, f32[1,80]{1,0:T(1,128)} %bitcast.12, f32[24,136,80]{2,1,0:T(8,128)} %bitcast.9), custom_call_target="tpu_custom_call" | custom-call | tf_op jit(solution)/shard_map/pack/pallas_call | solution.py:154
  4.0 12.0 %all-to-all-start = ((f32[32,88,128]{2,1,0:T(8,128)}), f32[32,88,128]{2,1,0:T(8,128)S(1)}, u32[]{:S(2)}, u32[]{:S(2)}) async-start(f32[32,88,128]{2,1,0:T(8,128)} %pack.1), calls=%async_computation | async-start | bytes 2883584 | tf_op jit(solution)/shard_map/all_to_all | solution.py:354
  16.0 5.7 %split_table.1.table_hbm = bf16[2,2,640,1280]{3,2,1,0:T(8,128)(2,1)} custom-call(f32[2,640,1280]{2,1,0:T(8,128)} %bitcast.8), custom_call_target="tpu_custom_call" | custom-call | tf_op jit(solution)/shard_map/split_table/pallas_call | solution.py:75
  21.8 0.0 copy-start.4
  21.8 0.0 copy-start
  21.8 0.0 copy-start.1
  21.8 0.0 copy-start.2
  21.8 0.0 copy-start.3
  21.8 28.3 %all-to-all-done.x_ref = f32[32,88,128]{2,1,0:T(8,128)S(1)} async-done(((f32[32,88,128]{2,1,0:T(8,128)}), f32[32,88,128]{2,1,0:T(8,128)S(1)}, u32[]{:S(2)}, u32[]{:S(2)}) %all-to-all-start) | async-done | bytes 1441824 | tf_op jit(solution)/shard_map/all_to_all | solution.py:354
  50.1 5.5 %legendre.1 = (f32[176,128]{1,0:T(8,128)S(1)}, f32[176,128]{1,0:T(8,128)S(1)}, f32[176,128]{1,0:T(8,128)S(1)}, f32[176,128]{1,0:T(8,128)S(1)}, f32[176,128]{1,0:...) custom-call(s32[2]{0:T(128)S(1)} %pad_add_fusion.where_ref.refs_0_, ...), custom_call_target="tpu_custom_call" | custom-call | tf_op jit(solution)/shard_map/legendre/pallas_call | solution.py:255
  55.6 3.7 %collective-permute-start = (f32[176,128]{1,0:T(8,128)S(1)}, f32[176,128]{1,0:T(8,128)S(1)}, u32[]{:S(2)}, u32[]{:S(2)}) collective-permute-start(f32[176,128]{1,0:T(8,128)S(1)} %get-tuple-element.14), channel_id=1, source_target_pairs={{0,1},{1,0},{2,3},{3,2},{4,5},{5,4},{6,7},{7,6},{8,9},{9,8},{10,11... | collective-permute-start | bytes 270344 | tf_op jit(solution)/shard_map/ppermute | solution.py:359
  59.3 1.2 %collective-permute-start.1 = (f32[176,128]{1,0:T(8,128)S(1)}, f32[176,128]{1,0:T(8,128)S(1)}, u32[]{:S(2)}, u32[]{:S(2)}) collective-permute-start(f32[176,128]{1,0:T(8,128)S(1)} %get-tuple-element.15), channel_id=1, source_target_pairs={{0,2},{1,3},{2,0},{3,1},{4,6},{5,7},{6,4},{7,5},{8,10},{9,11},{10,... | collective-permute-start | bytes 270344 | tf_op jit(solution)/shard_map/ppermute | solution.py:359
  60.6 0.5 collective-permute-start.2
  61.1 2.7 %collective-permute-start.3 = (f32[176,128]{1,0:T(8,128)S(1)}, f32[176,128]{1,0:T(8,128)S(1)}, u32[]{:S(2)}, u32[]{:S(2)}) collective-permute-start(f32[176,128]{1,0:T(8,128)S(1)} %get-tuple-element.17), channel_id=1, source_target_pairs={{0,4},{1,5},{2,6},{3,7},{4,0},{5,1},{6,2},{7,3},{8,12},{9,13},{10,... | collective-permute-start | bytes 270344 | tf_op jit(solution)/shard_map/ppermute | solution.py:359
  63.8 0.5 collective-permute-start.4
  64.3 0.0 collective-permute-done.refs_7_
  64.3 2.5 %collective-permute-start.5 = (f32[176,128]{1,0:T(8,128)S(1)}, f32[176,128]{1,0:T(8,128)S(1)}, u32[]{:S(2)}, u32[]{:S(2)}) collective-permute-start(f32[176,128]{1,0:T(8,128)S(1)} %get-tuple-element.19), channel_id=1, source_target_pairs={{0,6},{1,7},{2,4},{3,5},{4,2},{5,3},{6,0},{7,1},{8,14},{9,15},{10,... | collective-permute-start | bytes 270344 | tf_op jit(solution)/shard_map/ppermute | solution.py:359
  66.8 0.0 collective-permute-done.1.refs_8_
  66.8 0.5 collective-permute-start.6
  67.3 0.0 copy-done.4
  67.3 0.1 copy.10.refs_5_
  67.4 0.0 collective-permute-done.2.refs_9_
  67.4 2.1 %collective-permute-done.3.refs_10_ = f32[176,128]{1,0:T(8,128)S(1)} collective-permute-done((f32[176,128]{1,0:T(8,128)S(1)}, f32[176,128]{1,0:T(8,128)S(1)}, u32[]{:S(2)}, u32[]{:S(2)}) %collective-permute-start.3) | collective-permute-done | bytes 90144 | tf_op jit(solution)/shard_map/ppermute | solution.py:359
  69.5 2.3 %collective-permute-done.4.refs_11_ = f32[176,128]{1,0:T(8,128)S(1)} collective-permute-done((f32[176,128]{1,0:T(8,128)S(1)}, f32[176,128]{1,0:T(8,128)S(1)}, u32[]{:S(2)}, u32[]{:S(2)}) %collective-permute-start.4) | collective-permute-done | bytes 90144 | tf_op jit(solution)/shard_map/ppermute | solution.py:359
  71.8 1.6 %collective-permute-done.5.refs_12_ = f32[176,128]{1,0:T(8,128)S(1)} collective-permute-done((f32[176,128]{1,0:T(8,128)S(1)}, f32[176,128]{1,0:T(8,128)S(1)}, u32[]{:S(2)}, u32[]{:S(2)}) %collective-permute-start.5) | collective-permute-done | bytes 90144 | tf_op jit(solution)/shard_map/ppermute | solution.py:359
  73.4 1.9 %collective-permute-done.6.refs_13_ = f32[176,128]{1,0:T(8,128)S(1)} collective-permute-done((f32[176,128]{1,0:T(8,128)S(1)}, f32[176,128]{1,0:T(8,128)S(1)}, u32[]{:S(2)}, u32[]{:S(2)}) %collective-permute-start.6) | collective-permute-done | bytes 90144 | tf_op jit(solution)/shard_map/ppermute | solution.py:359
  75.3 0.0 copy-done
  75.3 0.0 copy-done.1
  75.3 0.0 copy-done.2
  75.4 0.0 copy-done.3
  75.4 3.1 %vertical.1 = f32[2,80,1088]{2,1,0:T(8,128)} custom-call(s32[2]{0:T(128)S(1)} %pad_add_fusion.where_ref.refs_0_, s32[24]{0:T(128)S(1)} %copy-done.3, f32[136,136]{1,0:T(8,128)S(1)} %copy-done, f32[136,136]{1,0:T(8,128)S(1)} %copy-done.1, f32[136,136]{1,0:T(8,128)S(1)} %copy-done.2, f32[136,1]{1,0:T(8,128)S(1)} %copy.10.refs_5_, ...), custom_call_target="tpu_custom_call" | custom-call | tf_op jit(solution)/shard_map/vertical/pallas_call | solution.py:322
Async XLA Ops:
  4.0 46.1 %all-to-all-start = ((f32[32,88,128]{2,1,0:T(8,128)}), f32[32,88,128]{2,1,0:T(8,128)S(1)}, u32[]{:S(2)}, u32[]{:S(2)}) async-start(f32[32,88,128]{2,1,0:T(8,128)} %pack.1), calls=%async_computation | async-start | bytes 2883584 | tf_op jit(solution)/shard_map/all_to_all | solution.py:354
  21.8 45.6 %copy-start.4 = (f32[136]{0:T(256)S(1)}, f32[136]{0:T(256)}, u32[]{:S(2)}) copy-start(f32[136]{0:T(256)} %param.16) | copy-start | bytes 1636
  21.8 53.6 %copy-start = (f32[136,136]{1,0:T(8,128)S(1)}, f32[136,136]{1,0:T(8,128)}, u32[]{:S(2)}) copy-start(f32[136,136]{1,0:T(8,128)} %refs_2_.1) | copy-start | bytes 221956
  21.8 53.6 %copy-start.1 = (f32[136,136]{1,0:T(8,128)S(1)}, f32[136,136]{1,0:T(8,128)}, u32[]{:S(2)}) copy-start(f32[136,136]{1,0:T(8,128)} %refs_3_.1) | copy-start | bytes 221956
  21.8 53.6 %copy-start.2 = (f32[136,136]{1,0:T(8,128)S(1)}, f32[136,136]{1,0:T(8,128)}, u32[]{:S(2)}) copy-start(f32[136,136]{1,0:T(8,128)} %refs_4_.1) | copy-start | bytes 221956
  21.8 53.6 %copy-start.3 = (s32[24]{0:T(128)S(1)}, s32[24]{0:T(128)}, u32[]{:S(2)}) copy-start(s32[24]{0:T(128)} %refs_1_.1) | copy-start | bytes 292
  55.6 8.7 %collective-permute-start = (f32[176,128]{1,0:T(8,128)S(1)}, f32[176,128]{1,0:T(8,128)S(1)}, u32[]{:S(2)}, u32[]{:S(2)}) collective-permute-start(f32[176,128]{1,0:T(8,128)S(1)} %get-tuple-element.14), channel_id=1, source_target_pairs={{0,1},{1,0},{2,3},{3,2},{4,5},{5,4},{6,7},{7,6},{8,9},{9,8},{10,11... | collective-permute-start | bytes 270344 | tf_op jit(solution)/shard_map/ppermute | solution.py:359
  59.3 7.5 %collective-permute-start.1 = (f32[176,128]{1,0:T(8,128)S(1)}, f32[176,128]{1,0:T(8,128)S(1)}, u32[]{:S(2)}, u32[]{:S(2)}) collective-permute-start(f32[176,128]{1,0:T(8,128)S(1)} %get-tuple-element.15), channel_id=1, source_target_pairs={{0,2},{1,3},{2,0},{3,1},{4,6},{5,7},{6,4},{7,5},{8,10},{9,11},{10,... | collective-permute-start | bytes 270344 | tf_op jit(solution)/shard_map/ppermute | solution.py:359
  60.6 6.9 %collective-permute-start.2 = (f32[176,128]{1,0:T(8,128)S(1)}, f32[176,128]{1,0:T(8,128)S(1)}, u32[]{:S(2)}, u32[]{:S(2)}) collective-permute-start(f32[176,128]{1,0:T(8,128)S(1)} %get-tuple-element.16), channel_id=1, source_target_pairs={{0,3},{1,2},{2,1},{3,0},{4,7},{5,6},{6,5},{7,4},{8,11},{9,10},{10,... | collective-permute-start | bytes 270344 | tf_op jit(solution)/shard_map/ppermute | solution.py:359
  61.1 8.4 %collective-permute-start.3 = (f32[176,128]{1,0:T(8,128)S(1)}, f32[176,128]{1,0:T(8,128)S(1)}, u32[]{:S(2)}, u32[]{:S(2)}) collective-permute-start(f32[176,128]{1,0:T(8,128)S(1)} %get-tuple-element.17), channel_id=1, source_target_pairs={{0,4},{1,5},{2,6},{3,7},{4,0},{5,1},{6,2},{7,3},{8,12},{9,13},{10,... | collective-permute-start | bytes 270344 | tf_op jit(solution)/shard_map/ppermute | solution.py:359
  63.8 8.0 %collective-permute-start.4 = (f32[176,128]{1,0:T(8,128)S(1)}, f32[176,128]{1,0:T(8,128)S(1)}, u32[]{:S(2)}, u32[]{:S(2)}) collective-permute-start(f32[176,128]{1,0:T(8,128)S(1)} %get-tuple-element.18), channel_id=1, source_target_pairs={{0,5},{1,4},{2,7},{3,6},{4,1},{5,0},{6,3},{7,2},{8,13},{9,12},{10,... | collective-permute-start | bytes 270344 | tf_op jit(solution)/shard_map/ppermute | solution.py:359
  64.3 9.1 %collective-permute-start.5 = (f32[176,128]{1,0:T(8,128)S(1)}, f32[176,128]{1,0:T(8,128)S(1)}, u32[]{:S(2)}, u32[]{:S(2)}) collective-permute-start(f32[176,128]{1,0:T(8,128)S(1)} %get-tuple-element.19), channel_id=1, source_target_pairs={{0,6},{1,7},{2,4},{3,5},{4,2},{5,3},{6,0},{7,1},{8,14},{9,15},{10,... | collective-permute-start | bytes 270344 | tf_op jit(solution)/shard_map/ppermute | solution.py:359
  66.8 8.5 %collective-permute-start.6 = (f32[176,128]{1,0:T(8,128)S(1)}, f32[176,128]{1,0:T(8,128)S(1)}, u32[]{:S(2)}, u32[]{:S(2)}) collective-permute-start(f32[176,128]{1,0:T(8,128)S(1)} %get-tuple-element.20), channel_id=1, source_target_pairs={{0,7},{1,6},{2,5},{3,4},{4,3},{5,2},{6,1},{7,0},{8,15},{9,14},{10,... | collective-permute-start | bytes 270344 | tf_op jit(solution)/shard_map/ppermute | solution.py:359

commit v4 on v2

v4 whole, which is shorter than its diff:
```python
import functools

import jax
import jax.numpy as jnp
from jax import lax
from jax.experimental import pallas as pl
from jax.experimental.pallas import tpu as pltpu
from jax.sharding import PartitionSpec as P


NTRUNC = 1280
LEVELS = 136
HALF = 64
F32 = jnp.float32
BF16 = jnp.bfloat16
VMEM = pltpu.VMEM


def whole():
    return pl.BlockSpec(memory_space=VMEM)


def smem():
    return pl.BlockSpec(memory_space=pltpu.SMEM)


def params(mb):
    return pltpu.CompilerParams(vmem_limit_bytes=mb << 20)


def lanes_of(shape):
    return lax.broadcasted_iota(jnp.int32, shape, 1)


def split(x):
    high = x.astype(BF16)
    low = (x - high.astype(F32)).astype(BF16)
    return high, low


def hbm():
    return pl.BlockSpec(memory_space=pltpu.HBM)


def stay(x):
    return pltpu.with_memory_space_constraint(x, pltpu.HBM)


def regroup_kernel(plan, *refs):
    count = len(refs) - len(plan)
    for out, picks in zip(refs[count:], plan):
        for n, (a, m) in enumerate(picks):
            out[n] = refs[a][m]


def regroup(arrays, plan):
    shape = [jax.ShapeDtypeStruct((len(picks),) + arrays[0].shape[1:], F32) for picks in plan]
    return pl.pallas_call(
        functools.partial(regroup_kernel, plan),
        out_shape=shape,
        in_specs=[whole()] * len(arrays),
        out_specs=[whole()] * len(plan),
        compiler_params=params(4),
    )(*arrays)


def load(refs):
    copies = [pltpu.make_async_copy(*r) for r in refs]
    for c in copies:
        c.start()
    for c in copies:
        c.wait()


def order_of(order, map_ref, slots):
    @pl.loop(0, slots)
    def _(s):
        order[s] = -1

    @pl.loop(0, map_ref.shape[0])
    def _(j):
        order[map_ref[j]] = j


def points_of(points, w, lat):
    first = w * lat
    row = first // 128
    off = first - row * 128
    lane = lanes_of((1, 128))
    back = lax.rem(128 - off, 128)
    here = pltpu.roll(points[pl.ds(row, 1), :], back, 1)
    after = pltpu.roll(points[pl.ds(jnp.minimum(row + 1, points.shape[0] - 1), 1), :], back, 1)
    return jnp.where(lane < 128 - off, here, after)[:, :lat]


def scaled(j, stride, points, weights, x):
    jj = jnp.maximum(j, 0)
    live = (2 * stride * jj < points) & (j >= 0)
    return x[jj] * jnp.where(live, weights, 0.0)


def two_up(x):
    y = jnp.transpose(x)
    half = y.shape[0] // 2
    return jnp.concatenate([y[:half], y[half:]], axis=1)


def pack_kernel(stride, first, sends, where_ref, map_hbm, points_hbm, weights_hbm, x_hbm, *rest):
    outs, (order, map_ref, pts, wts, x, sem) = rest[:-6], rest[-6:]
    cols = x.shape[1]
    load(
        [
            (points_hbm, pts, sem.at[0]),
            (weights_hbm, wts, sem.at[1]),
            (x_hbm.at[:, first : first + cols, :], x, sem.at[2]),
            (map_hbm, map_ref, sem.at[3]),
        ]
    )
    lat = x.shape[2]
    w = where_ref[0]
    order_of(order, map_ref, ZS * YS)
    points = points_of(pts, w, lat)
    weights = wts[...]
    y = w // ZS
    z = w - y * ZS
    for out, blocks in zip(outs, sends):
        for n, (d, k) in enumerate(blocks):
            s = ZS * lax.rem(y + k, YS) + lax.rem(z + d, ZS)
            v = scaled(order[s], stride, points, weights, x)
            out[n, 0:40, :] = two_up(v[:HALF])
            if cols > HALF:
                tail = jnp.concatenate([v[HALF:], jnp.zeros((8, 128 - lat), F32)], axis=1)
                out[n, 40:48, :] = tail


ZS, YS = 8, 4
FIRST_SENDS = [[(d, k) for d in ds for k in range(YS)] for ds in ((1, 3), (7, 5), (4,), (2,), (6,), (0,))]
Z_ORDER = (1, 3, 7, 5, 4, 2, 6, 0)
LAST_SENDS = [[(d, k) for d in Z_ORDER] for k in range(YS)]


def pack(where, slot_map, points, weights, x, stride, first, cols, sends):
    window, _, lat = x.shape
    rows = 40 if cols == HALF else 48
    out_shape = [jax.ShapeDtypeStruct((len(b), rows, 128), F32) for b in sends]
    return pl.pallas_call(
        lambda *r: pack_kernel(stride, first, sends, *r),
        out_shape=out_shape,
        in_specs=[smem(), hbm(), hbm(), hbm(), hbm()],
        out_specs=[whole()] * len(out_shape),
        scratch_shapes=[
            pltpu.SMEM((ZS * YS,), jnp.int32),
            pltpu.SMEM((window,), jnp.int32),
            VMEM(points.shape, jnp.int32),
            VMEM(weights.shape, F32),
            VMEM((window, cols, lat), F32),
            pltpu.SemaphoreType.DMA((4,)),
        ],
        compiler_params=params(8),
    )(where, stay(slot_map), stay(points), stay(weights), stay(x))


def flip_rows(x):
    rows = lax.broadcasted_iota(jnp.int32, (8, 128), 0)
    tiles = [
        jnp.take_along_axis(x[8 * t : 8 * t + 8], 7 - rows, axis=0) for t in reversed(range(x.shape[0] // 8))
    ]
    return jnp.concatenate(tiles, axis=0)


def pair_main(north, south):
    other = pltpu.roll(flip_rows(south), HALF, 1)
    return north + other, north - other


def high_low(x):
    high = x.astype(BF16).astype(F32)
    return high, x - high


def store_main(dst, p, w, packed):
    high, low = high_low(packed)
    left = lanes_of(high.shape) < HALF
    dst[p, pl.ds(80 * w, 40), 0:128] = jnp.where(left, high, pltpu.roll(low, HALF, 1))
    dst[p, pl.ds(80 * w + 40, 40), 0:128] = jnp.where(left, pltpu.roll(high, HALF, 1), low)


def fold(t, shift):
    return t + pltpu.roll(t, 128 - shift, 1)


def extra_columns(x_ref, rhs, half):
    zn = jnp.transpose(x_ref[0:half, 40:48, :].reshape(8 * half, 128))[:80]
    zs = flip_rows(jnp.transpose(x_ref[half:, 40:48, :].reshape(8 * half, 128))[:80])
    lane = lanes_of((8, 128))
    swap = 8 * (half - 1 - lane // 8) + lane % 8
    zs = jnp.concatenate([jnp.take_along_axis(zs[8 * t : 8 * t + 8], swap, axis=1) for t in range(10)], axis=0)
    even_group = (lanes_of((80, 128)) // 8) % 2 == 0
    for p, v in enumerate((zn + zs, zn - zs)):
        high, low = high_low(v)
        both = (
            jnp.where(even_group, high, pltpu.roll(low, 8, 1)),
            jnp.where(even_group, pltpu.roll(high, 120, 1), low),
        )
        for w in range(half):
            rhs[p, 80 * w : 80 * w + 80, 128:256] = pltpu.roll(both[w % 2], (128 - 16 * (w // 2)) % 128, 1)


STEPS, AHEAD = 2, 3


def legendre_kernel(places, wide, where_ref, *refs):
    if wide:
        arrays, (table_hbm, out_ref, keep) = refs[:-9], refs[-9:-6]
    else:
        members = 8
        arrays, (other_ref, keep), outs = refs[: -6 - members], refs[-6 - members : -4 - members], refs[-4 - members : -4]
    if wide:
        x_ref, rhs, rhsb, table, res, sem = refs[-6:]
    else:
        x_ref, rhs, rhsb, res = refs[-4:]
    count, step = keep.shape[0], keep.shape[2]
    each = count // 2

    def read(n):
        p = n // each
        at = pl.multiple_of((n - p * each) * step, 8)
        return pltpu.make_async_copy(table_hbm.at[p, pl.ds(at, step)], table.at[n], sem.at[n])

    if wide:
        for n in range(AHEAD):
            read(n).start()
    blocks = ZS * YS
    half = blocks // 2
    here = where_ref[0]
    me = where_ref[1]
    y = here // ZS
    z = here - ZS * y
    for a, n, d, k in places:
        source = ZS * lax.rem(y + YS - k, YS) + lax.rem(z + ZS - d, ZS)
        x_ref[source] = arrays[a][n]
    if wide:
        extra_columns(x_ref, rhs, half)

    @pl.loop(0, half, unroll=4)
    def _(w):
        for p, v in enumerate(pair_main(x_ref[w, 0:40, :], x_ref[blocks - 1 - w, 0:40, :])):
            store_main(rhs, p, w, v)

    for p in range(2):
        rhsb[p] = rhs[p].astype(BF16)

    @pl.loop(0, count)
    def _(n):
        if wide:

            @pl.when(n + AHEAD < count)
            def _():
                read(n + AHEAD).start()

            read(n).wait()
            high, low = split(table[n])
            keep[n, 0] = high
            keep[n, 1] = low
        p = n // each
        at = pl.multiple_of((n - p * each) * step, 8)
        both = keep[n].reshape(2 * step, keep.shape[3])
        o = jnp.dot(both, rhsb[p], preferred_element_type=F32)
        res[p, pl.ds(at, step), :] = o[:step] + o[step:]

    for r in range(8):
        mine = pl.ds(pl.multiple_of(80 * (me ^ r), 8), 80)
        e, o = fold(res[0, mine, 0:128], HALF), fold(res[1, mine, 0:128], HALF)
        main = jnp.where(lanes_of(e.shape) < HALF, e, o)
        if wide:
            out_ref[r, 0:80, :] = main
            ee, oo = fold(res[0, mine, 128:256], 8), fold(res[1, mine, 128:256], 8)
            extra = jnp.where(lanes_of(ee.shape) < 8, ee, pltpu.roll(oo, 8, 1))
            padded = jnp.concatenate([extra, jnp.zeros((48, 128), F32)], axis=0)
            out_ref[r, 80:96, :] = jnp.transpose(padded)[:16]
        else:
            outs[r][0:80, :] = main
            outs[r][80:176, :] = other_ref[r]


def legendre(where, arrays, places, table, members, other=None):
    wide = other is None
    lats = table.shape[-1]
    rows = table.shape[1] if wide else STEPS * table.shape[2]
    step = rows // STEPS
    shape = [jax.ShapeDtypeStruct((176, 128), F32)] * members
    lanes = 256 if wide else 128
    more = [] if wide else [other]
    return pl.pallas_call(
        functools.partial(legendre_kernel, places, wide),
        out_shape=[jax.ShapeDtypeStruct((members, 96, 128), F32), VMEM((2 * STEPS, 2, step, lats), BF16)] if wide else shape,
        in_specs=[smem()] + [whole()] * (len(arrays) + len(more)) + [hbm() if wide else whole()],
        out_specs=[whole()] * (2 if wide else members),
        scratch_shapes=[
            VMEM((ZS * YS,) + arrays[0].shape[1:], F32),
            VMEM((2, lats, lanes), F32),
            VMEM((2, lats, lanes), BF16),
        ]
        + [VMEM((2 * STEPS, step, lats), F32)] * wide
        + [VMEM((2, rows, lanes), F32)]
        + [pltpu.SemaphoreType.DMA((2 * STEPS,))] * wide,
        compiler_params=params(24),
    )(where, *arrays, *more, stay(table) if wide else pltpu.with_memory_space_constraint(table, pltpu.VMEM))


def dot3(a, b):
    ah, al = split(a)
    bh, bl = split(b)
    d = lambda u, v: jnp.dot(u, v, preferred_element_type=F32)
    return d(ah, bh) + (d(ah, bl) + d(al, bh))


def vertical_kernel(stride, where_ref, map_ref, to_ref, from_ref, thermal_ref, rates_ref, *refs):
    pieces, (out_ref, y) = refs[:-2], refs[-2:]
    here = where_ref[0]
    me = where_ref[1]
    row0 = 80 * me
    base = lax.fori_loop(
        0, map_ref.shape[0], lambda j, b: jnp.where(map_ref[j] == here, stride * j, b), jnp.int32(0)
    )
    lane = lanes_of((1, 128))
    degree = [base + 2 * (row0 + lane) + p for p in range(2)]
    live = [(d < NTRUNC) & (lane < 80) for d in degree]
    pad = jnp.zeros((48, 128), F32)
    for r, x in enumerate(pieces):
        at = pl.multiple_of(136 * (me ^ r), 8)
        for n in range(2):
            t = jnp.transpose(jnp.concatenate([x[80 * n : 80 * n + 80], pad], axis=0))
            for p in range(2):
                y[p, pl.ds(at + 64 * n, 64), :] = jnp.where(live[p], t[64 * p : 64 * p + 64], 0.0)
        for p in range(2):
            y[p, pl.ds(at + 128, 8), :] = jnp.where(live[p], x[160 + 8 * p : 168 + 8 * p], 0.0)
    div = jnp.concatenate(
        [y[p, pl.ds(2 + part, LEVELS, stride=8), :] for p in range(2) for part in range(2)], axis=1
    )
    modal = dot3(to_ref[...], div)
    damp = []
    for p in range(2):
        d = degree[p].astype(F32)
        ratio = d * (d + 1.0) / (NTRUNC * NTRUNC)
        damp.append(1.0 / (1.0 + rates_ref[...] * ratio))
    damped = modal * jnp.concatenate([damp[0], damp[0], damp[1], damp[1]], axis=1)
    new = dot3(from_ref[...], damped)
    heat = dot3(thermal_ref[...], new)
    for p in range(2):
        for part in range(2):
            at = 128 * (2 * p + part)
            y[p, pl.ds(2 + part, LEVELS, stride=8), :] = new[:, at : at + 128]
            t = y[p, pl.ds(4 + part, LEVELS, stride=8), :]
            y[p, pl.ds(4 + part, LEVELS, stride=8), :] = t - heat[:, at : at + 128]
    for p in range(2):
        for c in range(8):
            out_ref[p, :, 128 * c : 128 * c + 128] = jnp.transpose(y[p, 128 * c : 128 * c + 128, :])[:80]
        tail = jnp.concatenate([y[p, 1024:1088, :], jnp.zeros((64, 128), F32)], axis=0)
        out_ref[p, :, 1024:1088] = jnp.transpose(tail)[:80, :64]


def vertical(where, slot_map, to_modes, from_modes, thermal, rates, pieces, stride):
    return pl.pallas_call(
        lambda *refs: vertical_kernel(stride, *refs),
        out_shape=jax.ShapeDtypeStruct((2, 80, 8 * LEVELS), F32),
        in_specs=[smem(), smem()] + [whole()] * (4 + len(pieces)),
        out_specs=whole(),
        scratch_shapes=[VMEM((2, 8 * LEVELS, 128), F32)],
        compiler_params=params(12),
        name="vertical",
    )(where, slot_map, to_modes, from_modes, thermal, rates, *pieces)


def shift(v, axis, move, size):
    return lax.ppermute(v, axis, [(i, move(i)) for i in range(size)])


def along_z(v, d):
    return shift(v, "wave", lambda i: i // 8 * 8 + (i + d) % 8, 32)


def along_y(v, d):
    return shift(v, "wave", lambda i: (i + 8 * d) % 32, 32)


def on_device(
    fourier,
    weights,
    row_points,
    slot_map,
    legendre_lookup,
    to_modes,
    from_modes,
    mode_rates,
    thermal_response_matrix,
):
    members = lax.axis_size("lev")
    w = lax.axis_index("wave")
    l = lax.axis_index("lev")
    lat, window, _ = fourier.shape
    stride = NTRUNC // window
    where = jnp.stack([w, l]).astype(jnp.int32)
    x = jnp.transpose(fourier, (1, 2, 0))
    points = row_points.reshape(-1, 128)
    wts = weights.reshape(1, lat)
    s1, s7, s4, s2, s6, s0 = pack(where, slot_map, points, wts, x, stride, HALF, 72, FIRST_SENDS)
    r1 = along_z(s1, 1)
    r7 = along_z(s7, -1)
    p4 = along_z(s4, 4)
    ls = pack(where, slot_map, points, wts, x, stride, 0, HALF, LAST_SENDS)
    lr = [ls[0]] + [along_y(ls[d], d) for d in (1, 2, 3)]
    table = legendre_lookup[0]
    (o2,) = regroup([s2, r1], [[(0, n) for n in range(4)] + [(1, 4 + n) for n in range(4)]])
    p2 = along_z(o2, 2)
    (o6,) = regroup([s6, r7], [[(0, n) for n in range(4)] + [(1, 4 + n) for n in range(4)]])
    m2 = along_z(o6, -2)
    spots = [(5, 0), (0, 0), (3, 0), (3, 4), (2, 0), (4, 4), (4, 0), (1, 0)]
    got = [r1, r7, p4, p2, m2, s0]
    fo = regroup(got, [[(a, n + d) for a, n in spots] for d in (1, 2, 3)])
    fy = [along_y(v, d) for d, v in zip((1, 2, 3), fo)]
    places = [(a, n, d, 0) for d, (a, n) in enumerate(spots)]
    places += [(5 + k, d, d, k) for k in (1, 2, 3) for d in range(ZS)]

    pick = lambda *ds: [(k, Z_ORDER.index(d)) for d in ds for k in range(YS)]
    g1, g7, g4 = regroup(lr, [pick(1, 3), pick(7, 5), pick(4)])
    l1 = along_z(g1, 1)
    l7 = along_z(g7, -1)
    l4 = along_z(g4, 4)
    (g2,) = regroup(lr + [l1], [pick(2) + [(4, 4 + n) for n in range(4)]])
    (g6,) = regroup(lr + [l7], [pick(6) + [(4, 4 + n) for n in range(4)]])
    l2 = along_z(g2, 2)
    l6 = along_z(g6, -2)

    f, table = legendre(where, got + fy, places, table, members)
    spots = [(1, 0, 1), (2, 0, 7), (3, 0, 4), (4, 0, 2), (4, 4, 3), (5, 0, 6), (5, 4, 5)]
    places = [(a, n + k, d, k) for a, n, d in spots for k in range(YS)]
    last = len(Z_ORDER) - 1
    places += [(0 if k == 0 else 5 + k, last, 0, k) for k in range(YS)]
    local = legendre(where, [ls[0], l1, l7, l4, l2, l6] + lr[1:], places, table, members, f)
    mine = [local[0]]
    for r in range(1, members):
        mine.append(lax.ppermute(local[r], "lev", [(i, i ^ r) for i in range(members)]))
    rates = mode_rates.reshape(-1, 1)
    out = vertical(where, slot_map, to_modes, from_modes, thermal_response_matrix, rates, mine, stride)
    return out[None]


def solution(mesh):
    placed = (
        P("wave", None, "lev"),
        P("wave"),
        P(),
        P(),
        P("wave", None, None, None),
        P(),
        P(),
        P(),
        P(),
    )
    return jax.shard_map(
        on_device,
        mesh=mesh,
        in_specs=placed,
        out_specs=P("wave", None, "lev", None),
        check_vma=False,
    )
```

time: 80.7 us -> 80 us (level)
  starting transfers between devices: 20 us -> 42.4 us
  waiting for transfers between devices: 39.7 us -> 17.8 us
  Pallas kernels: 20.5 us -> 19.1 us
    ppermute x0 -> x23, starting transfers between devices: none -> 42.4 us  [the longest x16 29.3 us: shift(): return lax.ppermute(v, axis, [(i, move(i)) for i in range(size)])]
    all_to_all x2 -> x0, waiting for transfers between devices: 39.7 us -> none  [the longest x1 28.3 us: on_device(): lax.all_to_all(sent, 'wave', split_axis=0, concat_axis=0, tiled=True)]
    all_to_all x2 -> x0, starting transfers between devices: 20 us -> none  [the longest x1 12 us: on_device(): lax.all_to_all(sent, 'wave', split_axis=0, concat_axis=0, tiled=True)]
    ppermute x0 -> x23, waiting for transfers between devices: none -> 17.8 us  [the longest x16 9.91 us: shift(): return lax.ppermute(v, axis, [(i, move(i)) for i in range(size)])]
    pallas_call x3 -> x10, Pallas kernels: 17.5 us -> 16 us  [the longest x2 10.1 us: legendre(): pl.pallas_call(functools.partial(legendre_kernel, places, wide), out_shap...]
  transfers between devices with their start and end apart: 2 -> 23, of which waited for: 2 -> 9; matrix products, arithmetic and copies ran while one was open for 0% -> 0% of each run, Pallas kernels for 7% -> 11%
where the time goes in v4:
time: 80 us; the launch traced here: 79.8 us
  starting transfers between devices  42.4 us (53%)
  Pallas kernels  19.1 us (24%)
  waiting for transfers between devices  17.8 us (22%)
    ppermute x16, starting transfers between devices, shift(): return lax.ppermute(v, axis, [(i, move(i)) for i in range(size)])  29.3 us
    ppermute x7, starting transfers between devices, on_device(): lax.ppermute(local[r], 'lev', [(i, i ^ r) for i in range(members)])  13.1 us
    pallas_call x2, Pallas kernels, legendre(): pl.pallas_call(functools.partial(legendre_kernel, places, wide), out_shap...  10.1 us
    ppermute x16, waiting for transfers between devices, shift(): return lax.ppermute(v, axis, [(i, move(i)) for i in range(size)])  9.91 us
    ppermute x7, waiting for transfers between devices, on_device(): lax.ppermute(local[r], 'lev', [(i, i ^ r) for i in range(members)])  7.92 us
    pallas_call x2, Pallas kernels, pack(): pl.pallas_call(lambda *r: pack_kernel(stride, first, sends, *r), out_shap...  5.78 us
    pallas_call x1, Pallas kernels, vertical(): pl.pallas_call(lambda *refs: vertical_kernel(stride, *refs), out_shape=ja...  3.11 us
  transfers between devices with their start and end apart: 23, of which 9 were waited for; matrix products, arithmetic and copies ran while one was open for 0% of the time, Pallas kernels for 11%

profile of v4, /device:TPU:1, one launch (start us, length us, event | category | flops | bytes accessed | tf_op | source)
XLA Modules:
  0.0 79.8 jit_solution(3541511853719679324)
XLA Ops:
  0.0 0.1 pad_add_fusion.r_0_.where_ref.refs_0_
  0.1 2.9 %shard_map.95 = (f32[8,48,128]{2,1,0:T(8,128)S(1)}, f32[8,48,128]{2,1,0:T(8,128)S(1)}, f32[4,48,128]{2,1,0:T(8,128)S(1)}, f32[4,48,128]{2,1,0:T(8,128)S(1)}, f32...) custom-call(s32[2]{0:T(128)S(1)} %pad_add_fusion.r_0_.where_ref.refs_0_, s32[24]{0:T(128)} %refs_1_.1, ...), custom_call_target="tpu_custom_call" | custom-call | tf_op jit(solution)/shard_map/pallas_call | solution.py:146
  3.0 2.5 %collective-permute-start.8 = (f32[8,48,128]{2,1,0:T(8,128)S(1)}, f32[8,48,128]{2,1,0:T(8,128)S(1)}, u32[]{:S(2)}, u32[]{:S(2)}) collective-permute-start(f32[8,48,128]{2,1,0:T(8,128)S(1)} %get-tuple-element.38), channel_id=1, source_target_pairs={{0,8},{8,16},{16,24},{24,32},{32,40},{40,48},{48,56},{56,0},{64,72... | collective-permute-start | bytes 589832 | tf_op jit(solution)/shard_map/ppermute | solution.py:376
  5.5 4.0 %collective-permute-start.9 = (f32[8,48,128]{2,1,0:T(8,128)S(1)}, f32[8,48,128]{2,1,0:T(8,128)S(1)}, u32[]{:S(2)}, u32[]{:S(2)}) collective-permute-start(f32[8,48,128]{2,1,0:T(8,128)S(1)} %get-tuple-element.39), channel_id=1, source_target_pairs={{0,56},{8,0},{16,8},{24,16},{32,24},{40,32},{48,40},{56,48},{64,12... | collective-permute-start | bytes 589832 | tf_op jit(solution)/shard_map/ppermute | solution.py:376
  9.6 2.9 %shard_map.91 = (f32[8,40,128]{2,1,0:T(8,128)S(1)}, f32[8,40,128]{2,1,0:T(8,128)S(1)}, f32[8,40,128]{2,1,0:T(8,128)S(1)}, f32[8,40,128]{2,1,0:T(8,128)S(1)}) custom-call(s32[2]{0:T(128)S(1)} %pad_add_fusion.r_0_.where_ref.refs_0_, s32[24]{0:T(128)} %refs_1_.1, s32[20,128]{1,0:T(8,128)} %bitcast.12, f32[1,80]{1,0:T(1,128)} %bitcast.14, f32[24,136,80]{2,1,0:T(8,128)} %bitcast.9), custom_call_target="tpu_custom_call" | custom-call | tf_op jit(solution)/shard_map/pallas_call | solution.py:146
  12.4 1.4 %collective-permute-start = (f32[8,40,128]{2,1,0:T(8,128)S(1)}, f32[8,40,128]{2,1,0:T(8,128)S(1)}, u32[]{:S(2)}, u32[]{:S(2)}) collective-permute-start(f32[8,40,128]{2,1,0:T(8,128)S(1)} %get-tuple-element.32), channel_id=1, source_target_pairs={{0,64},{8,72},{16,80},{24,88},{32,96},{40,104},{48,112},{56,120},{... | collective-permute-start | bytes 491528 | tf_op jit(solution)/shard_map/ppermute | solution.py:376
  13.8 2.6 %collective-permute-start.1 = (f32[8,40,128]{2,1,0:T(8,128)S(1)}, f32[8,40,128]{2,1,0:T(8,128)S(1)}, u32[]{:S(2)}, u32[]{:S(2)}) collective-permute-start(f32[8,40,128]{2,1,0:T(8,128)S(1)} %get-tuple-element.33), channel_id=1, source_target_pairs={{0,128},{8,136},{16,144},{24,152},{32,160},{40,168},{48,176},{56,1... | collective-permute-start | bytes 491528 | tf_op jit(solution)/shard_map/ppermute | solution.py:376
  16.4 1.1 %collective-permute-start.2 = (f32[8,40,128]{2,1,0:T(8,128)S(1)}, f32[8,40,128]{2,1,0:T(8,128)S(1)}, u32[]{:S(2)}, u32[]{:S(2)}) collective-permute-start(f32[8,40,128]{2,1,0:T(8,128)S(1)} %get-tuple-element.34), channel_id=1, source_target_pairs={{0,192},{8,200},{16,208},{24,216},{32,224},{40,232},{48,240},{56,2... | collective-permute-start | bytes 491528 | tf_op jit(solution)/shard_map/ppermute | solution.py:376
  17.5 0.0 collective-permute-done.8.refs_1_.refs_0_
  17.5 0.1 collective-permute-start.11
  17.6 0.0 collective-permute-done.9.refs_1_
  17.6 3.6 %collective-permute-start.12 = (f32[8,48,128]{2,1,0:T(8,128)S(1)}, f32[8,48,128]{2,1,0:T(8,128)S(1)}, u32[]{:S(2)}, u32[]{:S(2)}) collective-permute-start(f32[8,48,128]{2,1,0:T(8,128)S(1)} %shard_map.97), channel_id=1, source_target_pairs={{0,48},{8,56},{16,0},{24,8},{32,16},{40,24},{48,32},{56,40},{64,11... | collective-permute-start | bytes 589832 | tf_op jit(solution)/shard_map/ppermute | solution.py:376
  21.3 0.0 collective-permute-done.refs_1_.refs_6_
  21.3 3.9 %collective-permute-start.10 = (f32[4,48,128]{2,1,0:T(8,128)S(1)}, f32[4,48,128]{2,1,0:T(8,128)S(1)}, u32[]{:S(2)}, u32[]{:S(2)}) collective-permute-start(f32[4,48,128]{2,1,0:T(8,128)S(1)} %get-tuple-element.40), channel_id=1, source_target_pairs={{0,32},{8,40},{16,48},{24,56},{32,0},{40,8},{48,16},{56,24},{64,96... | collective-permute-start | bytes 294920 | tf_op jit(solution)/shard_map/ppermute | solution.py:376
  25.2 0.0 collective-permute-done.1.refs_2_.refs_7_
  25.2 0.0 collective-permute-done.2.refs_3_.refs_8_
  25.2 0.1 collective-permute-start.4
  25.3 1.5 %collective-permute-start.3 = (f32[8,40,128]{2,1,0:T(8,128)S(1)}, f32[8,40,128]{2,1,0:T(8,128)S(1)}, u32[]{:S(2)}, u32[]{:S(2)}) collective-permute-start(f32[8,40,128]{2,1,0:T(8,128)S(1)} %get-tuple-element.35), channel_id=1, source_target_pairs={{0,8},{8,16},{16,24},{24,32},{32,40},{40,48},{48,56},{56,0},{64,72... | collective-permute-start | bytes 491528 | tf_op jit(solution)/shard_map/ppermute | solution.py:376
  26.8 4.7 %collective-permute-done.10.refs_2_ = f32[4,48,128]{2,1,0:T(8,128)S(1)} collective-permute-done((f32[4,48,128]{2,1,0:T(8,128)S(1)}, f32[4,48,128]{2,1,0:T(8,128)S(1)}, u32[]{:S(2)}, u32[]{:S(2)}) %collective-permute-start.10) | collective-permute-done | bytes 98336 | tf_op jit(solution)/shard_map/ppermute | solution.py:376
  31.5 0.0 collective-permute-done.11.refs_3_
  31.5 1.6 %collective-permute-done.12.refs_4_ = f32[8,48,128]{2,1,0:T(8,128)S(1)} collective-permute-done((f32[8,48,128]{2,1,0:T(8,128)S(1)}, f32[8,48,128]{2,1,0:T(8,128)S(1)}, u32[]{:S(2)}, u32[]{:S(2)}) %collective-permute-start.12) | collective-permute-done | bytes 196640 | tf_op jit(solution)/shard_map/ppermute | solution.py:376
  33.1 0.5 collective-permute-start.13
  33.6 1.8 %collective-permute-start.14 = (f32[8,48,128]{2,1,0:T(8,128)S(1)}, f32[8,48,128]{2,1,0:T(8,128)S(1)}, u32[]{:S(2)}, u32[]{:S(2)}) collective-permute-start(f32[8,48,128]{2,1,0:T(8,128)S(1)} %get-tuple-element.45), channel_id=1, source_target_pairs={{0,128},{8,136},{16,144},{24,152},{32,160},{40,168},{48,176},{56,1... | collective-permute-start | bytes 589832 | tf_op jit(solution)/shard_map/ppermute | solution.py:376
  35.4 0.7 collective-permute-start.15
  36.1 1.2 %collective-permute-done.4.refs_4_.refs_2_ = f32[8,40,128]{2,1,0:T(8,128)S(1)} collective-permute-done((f32[8,40,128]{2,1,0:T(8,128)S(1)}, f32[8,40,128]{2,1,0:T(8,128)S(1)}, u32[]{:S(2)}, u32[]{:S(2)}) %collective-permute-start.4) | collective-permute-done | bytes 163872 | tf_op jit(solution)/shard_map/ppermute | solution.py:376
  37.3 2.8 %collective-permute-start.7 = (f32[8,40,128]{2,1,0:T(8,128)S(1)}, f32[8,40,128]{2,1,0:T(8,128)S(1)}, u32[]{:S(2)}, u32[]{:S(2)}) collective-permute-start(f32[8,40,128]{2,1,0:T(8,128)S(1)} %shard_map.94), channel_id=1, source_target_pairs={{0,48},{8,56},{16,0},{24,8},{32,16},{40,24},{48,32},{56,40},{64,11... | collective-permute-start | bytes 491528 | tf_op jit(solution)/shard_map/ppermute | solution.py:376
  40.2 0.0 collective-permute-done.3.refs_4_.refs_1_
  40.2 0.3 collective-permute-start.6
  40.4 0.0 collective-permute-done.13.refs_6_
  40.5 2.5 %collective-permute-start.5 = (f32[4,40,128]{2,1,0:T(8,128)S(1)}, f32[4,40,128]{2,1,0:T(8,128)S(1)}, u32[]{:S(2)}, u32[]{:S(2)}) collective-permute-start(f32[4,40,128]{2,1,0:T(8,128)S(1)} %get-tuple-element.37), channel_id=1, source_target_pairs={{0,32},{8,40},{16,48},{24,56},{32,0},{40,8},{48,16},{56,24},{64,96... | collective-permute-start | bytes 245768 | tf_op jit(solution)/shard_map/ppermute | solution.py:376
  42.9 0.2 collective-permute-done.14.refs_7_
  43.2 0.0 collective-permute-done.15.refs_8_
  43.2 0.0 copy-start.4
  43.2 0.0 copy-start
  43.2 0.0 copy-start.1
  43.2 0.0 copy-start.2
  43.2 0.0 copy-start.3
  43.2 5.9 %shard_map.99 = (f32[8,96,128]{2,1,0:T(8,128)S(1)}, bf16[4,2,320,1280]{3,2,1,0:T(8,128)(2,1)S(1)}) custom-call(s32[2]{0:T(128)S(1)} %pad_add_fusion.r_0_.where_ref.refs_0_, f32[8,48,128]{2,1,0:T(8,128)S(1)} %collective-permute-done.8.refs_1_.refs_0_, f32[8,48,128]{2,1,0:T(8,128)S(1)} %collective-permute-done.9.refs_1_, ...), custom_call_target="tpu_custom_call" | custom-call | tf_op jit(solution)/shard_map/pallas_call | solution.py:294
  49.1 0.0 collective-permute-done.5.refs_3_
  49.1 0.0 collective-permute-done.7.refs_5_
  49.1 2.1 %collective-permute-done.6.refs_4_ = f32[8,40,128]{2,1,0:T(8,128)S(1)} collective-permute-done((f32[8,40,128]{2,1,0:T(8,128)S(1)}, f32[8,40,128]{2,1,0:T(8,128)S(1)}, u32[]{:S(2)}, u32[]{:S(2)}) %collective-permute-start.6) | collective-permute-done | bytes 163872 | tf_op jit(solution)/shard_map/ppermute | solution.py:376
  51.3 4.2 %shard_map.100 = (f32[176,128]{1,0:T(8,128)S(1)}, f32[176,128]{1,0:T(8,128)S(1)}, f32[176,128]{1,0:T(8,128)S(1)}, f32[176,128]{1,0:T(8,128)S(1)}, f32[176,128]{1...) custom-call(s32[2]{0:T(128)S(1)} %pad_add_fusion.r_0_.where_ref.refs_0_, ...), custom_call_target="tpu_custom_call" | custom-call | tf_op jit(solution)/shard_map/pallas_call | solution.py:294
  55.5 5.2 %collective-permute-start.16 = (f32[176,128]{1,0:T(8,128)S(1)}, f32[176,128]{1,0:T(8,128)S(1)}, u32[]{:S(2)}, u32[]{:S(2)}) collective-permute-start(f32[176,128]{1,0:T(8,128)S(1)} %get-tuple-element.50), channel_id=1, source_target_pairs={{0,1},{1,0},{2,3},{3,2},{4,5},{5,4},{6,7},{7,6},{8,9},{9,8},{10,11... | collective-permute-start | bytes 270344 | tf_op jit(solution)/shard_map/ppermute | solution.py:443
  60.6 1.2 %collective-permute-start.17 = (f32[176,128]{1,0:T(8,128)S(1)}, f32[176,128]{1,0:T(8,128)S(1)}, u32[]{:S(2)}, u32[]{:S(2)}) collective-permute-start(f32[176,128]{1,0:T(8,128)S(1)} %get-tuple-element.51), channel_id=1, source_target_pairs={{0,2},{1,3},{2,0},{3,1},{4,6},{5,7},{6,4},{7,5},{8,10},{9,11},{10,... | collective-permute-start | bytes 270344 | tf_op jit(solution)/shard_map/ppermute | solution.py:443
  61.8 0.5 collective-permute-start.18
  62.4 2.7 %collective-permute-start.19 = (f32[176,128]{1,0:T(8,128)S(1)}, f32[176,128]{1,0:T(8,128)S(1)}, u32[]{:S(2)}, u32[]{:S(2)}) collective-permute-start(f32[176,128]{1,0:T(8,128)S(1)} %get-tuple-element.53), channel_id=1, source_target_pairs={{0,4},{1,5},{2,6},{3,7},{4,0},{5,1},{6,2},{7,3},{8,12},{9,13},{10,... | collective-permute-start | bytes 270344 | tf_op jit(solution)/shard_map/ppermute | solution.py:443
  65.1 0.5 collective-permute-start.20
  65.6 0.0 collective-permute-done.16.refs_7_
  65.6 2.5 %collective-permute-start.21 = (f32[176,128]{1,0:T(8,128)S(1)}, f32[176,128]{1,0:T(8,128)S(1)}, u32[]{:S(2)}, u32[]{:S(2)}) collective-permute-start(f32[176,128]{1,0:T(8,128)S(1)} %get-tuple-element.55), channel_id=1, source_target_pairs={{0,6},{1,7},{2,4},{3,5},{4,2},{5,3},{6,0},{7,1},{8,14},{9,15},{10,... | collective-permute-start | bytes 270344 | tf_op jit(solution)/shard_map/ppermute | solution.py:443
  68.1 0.0 collective-permute-done.17.refs_8_
  68.1 0.5 collective-permute-start.22
  68.6 0.0 copy-done.4
  68.6 0.1 copy.10.refs_5_
  68.7 0.0 collective-permute-done.18.refs_9_
  68.7 2.1 %collective-permute-done.19.refs_10_ = f32[176,128]{1,0:T(8,128)S(1)} collective-permute-done((f32[176,128]{1,0:T(8,128)S(1)}, f32[176,128]{1,0:T(8,128)S(1)}, u32[]{:S(2)}, u32[]{:S(2)}) %collective-permute-start.19) | collective-permute-done | bytes 90144 | tf_op jit(solution)/shard_map/ppermute | solution.py:443
  70.8 2.3 %collective-permute-done.20.refs_11_ = f32[176,128]{1,0:T(8,128)S(1)} collective-permute-done((f32[176,128]{1,0:T(8,128)S(1)}, f32[176,128]{1,0:T(8,128)S(1)}, u32[]{:S(2)}, u32[]{:S(2)}) %collective-permute-start.20) | collective-permute-done | bytes 90144 | tf_op jit(solution)/shard_map/ppermute | solution.py:443
  73.1 1.6 %collective-permute-done.21.refs_12_ = f32[176,128]{1,0:T(8,128)S(1)} collective-permute-done((f32[176,128]{1,0:T(8,128)S(1)}, f32[176,128]{1,0:T(8,128)S(1)}, u32[]{:S(2)}, u32[]{:S(2)}) %collective-permute-start.21) | collective-permute-done | bytes 90144 | tf_op jit(solution)/shard_map/ppermute | solution.py:443
  74.7 1.9 %collective-permute-done.22.refs_13_ = f32[176,128]{1,0:T(8,128)S(1)} collective-permute-done((f32[176,128]{1,0:T(8,128)S(1)}, f32[176,128]{1,0:T(8,128)S(1)}, u32[]{:S(2)}, u32[]{:S(2)}) %collective-permute-start.22) | collective-permute-done | bytes 90144 | tf_op jit(solution)/shard_map/ppermute | solution.py:443
  76.6 0.0 copy-done
  76.6 0.0 copy-done.1
  76.6 0.0 copy-done.2
  76.6 0.0 copy-done.3
  76.6 3.1 %vertical.1 = f32[2,80,1088]{2,1,0:T(8,128)} custom-call(s32[2]{0:T(128)S(1)} %pad_add_fusion.r_0_.where_ref.refs_0_, s32[24]{0:T(128)S(1)} %copy-done.3, f32[136,136]{1,0:T(8,128)S(1)} %copy-done, f32[136,136]{1,0:T(8,128)S(1)} %copy-done.1, f32[136,136]{1,0:T(8,128)S(1)} %copy-done.2, f32[136,1]{1,0:T(8,128)S(1)} %copy.10.refs_5_, ...), custom_call_target="tpu_custom_call" | custom-call | tf_op jit(solution)/shard_map/vertical/pallas_call | solution.py:364
  (6 shorter events, 0.1 us)
Async XLA Ops:
  3.0 14.5 %collective-permute-start.8 = (f32[8,48,128]{2,1,0:T(8,128)S(1)}, f32[8,48,128]{2,1,0:T(8,128)S(1)}, u32[]{:S(2)}, u32[]{:S(2)}) collective-permute-start(f32[8,48,128]{2,1,0:T(8,128)S(1)} %get-tuple-element.38), channel_id=1, source_target_pairs={{0,8},{8,16},{16,24},{24,32},{32,40},{40,48},{48,56},{56,0},{64,72... | collective-permute-start | bytes 589832 | tf_op jit(solution)/shard_map/ppermute | solution.py:376
  5.5 12.1 %collective-permute-start.9 = (f32[8,48,128]{2,1,0:T(8,128)S(1)}, f32[8,48,128]{2,1,0:T(8,128)S(1)}, u32[]{:S(2)}, u32[]{:S(2)}) collective-permute-start(f32[8,48,128]{2,1,0:T(8,128)S(1)} %get-tuple-element.39), channel_id=1, source_target_pairs={{0,56},{8,0},{16,8},{24,16},{32,24},{40,32},{48,40},{56,48},{64,12... | collective-permute-start | bytes 589832 | tf_op jit(solution)/shard_map/ppermute | solution.py:376
  12.4 8.8 %collective-permute-start = (f32[8,40,128]{2,1,0:T(8,128)S(1)}, f32[8,40,128]{2,1,0:T(8,128)S(1)}, u32[]{:S(2)}, u32[]{:S(2)}) collective-permute-start(f32[8,40,128]{2,1,0:T(8,128)S(1)} %get-tuple-element.32), channel_id=1, source_target_pairs={{0,64},{8,72},{16,80},{24,88},{32,96},{40,104},{48,112},{56,120},{... | collective-permute-start | bytes 491528 | tf_op jit(solution)/shard_map/ppermute | solution.py:376
  13.8 11.4 %collective-permute-start.1 = (f32[8,40,128]{2,1,0:T(8,128)S(1)}, f32[8,40,128]{2,1,0:T(8,128)S(1)}, u32[]{:S(2)}, u32[]{:S(2)}) collective-permute-start(f32[8,40,128]{2,1,0:T(8,128)S(1)} %get-tuple-element.33), channel_id=1, source_target_pairs={{0,128},{8,136},{16,144},{24,152},{32,160},{40,168},{48,176},{56,1... | collective-permute-start | bytes 491528 | tf_op jit(solution)/shard_map/ppermute | solution.py:376
  16.4 8.8 %collective-permute-start.2 = (f32[8,40,128]{2,1,0:T(8,128)S(1)}, f32[8,40,128]{2,1,0:T(8,128)S(1)}, u32[]{:S(2)}, u32[]{:S(2)}) collective-permute-start(f32[8,40,128]{2,1,0:T(8,128)S(1)} %get-tuple-element.34), channel_id=1, source_target_pairs={{0,192},{8,200},{16,208},{24,216},{32,224},{40,232},{48,240},{56,2... | collective-permute-start | bytes 491528 | tf_op jit(solution)/shard_map/ppermute | solution.py:376
  17.5 13.9 %collective-permute-start.11 = (f32[8,48,128]{2,1,0:T(8,128)S(1)}, f32[8,48,128]{2,1,0:T(8,128)S(1)}, u32[]{:S(2)}, u32[]{:S(2)}) collective-permute-start(f32[8,48,128]{2,1,0:T(8,128)S(1)} %shard_map.96), channel_id=1, source_target_pairs={{0,16},{8,24},{16,32},{24,40},{32,48},{40,56},{48,0},{56,8},{64,80... | collective-permute-start | bytes 589832 | tf_op jit(solution)/shard_map/ppermute | solution.py:376
  17.6 15.4 %collective-permute-start.12 = (f32[8,48,128]{2,1,0:T(8,128)S(1)}, f32[8,48,128]{2,1,0:T(8,128)S(1)}, u32[]{:S(2)}, u32[]{:S(2)}) collective-permute-start(f32[8,48,128]{2,1,0:T(8,128)S(1)} %shard_map.97), channel_id=1, source_target_pairs={{0,48},{8,56},{16,0},{24,8},{32,16},{40,24},{48,32},{56,40},{64,11... | collective-permute-start | bytes 589832 | tf_op jit(solution)/shard_map/ppermute | solution.py:376
  21.3 10.2 %collective-permute-start.10 = (f32[4,48,128]{2,1,0:T(8,128)S(1)}, f32[4,48,128]{2,1,0:T(8,128)S(1)}, u32[]{:S(2)}, u32[]{:S(2)}) collective-permute-start(f32[4,48,128]{2,1,0:T(8,128)S(1)} %get-tuple-element.40), channel_id=1, source_target_pairs={{0,32},{8,40},{16,48},{24,56},{32,0},{40,8},{48,16},{56,24},{64,96... | collective-permute-start | bytes 294920 | tf_op jit(solution)/shard_map/ppermute | solution.py:376
  25.2 12.1 %collective-permute-start.4 = (f32[8,40,128]{2,1,0:T(8,128)S(1)}, f32[8,40,128]{2,1,0:T(8,128)S(1)}, u32[]{:S(2)}, u32[]{:S(2)}) collective-permute-start(f32[8,40,128]{2,1,0:T(8,128)S(1)} %get-tuple-element.36), channel_id=1, source_target_pairs={{0,56},{8,0},{16,8},{24,16},{32,24},{40,32},{48,40},{56,48},{64,12... | collective-permute-start | bytes 491528 | tf_op jit(solution)/shard_map/ppermute | solution.py:376
  25.3 14.8 %collective-permute-start.3 = (f32[8,40,128]{2,1,0:T(8,128)S(1)}, f32[8,40,128]{2,1,0:T(8,128)S(1)}, u32[]{:S(2)}, u32[]{:S(2)}) collective-permute-start(f32[8,40,128]{2,1,0:T(8,128)S(1)} %get-tuple-element.35), channel_id=1, source_target_pairs={{0,8},{8,16},{16,24},{24,32},{32,40},{40,48},{48,56},{56,0},{64,72... | collective-permute-start | bytes 491528 | tf_op jit(solution)/shard_map/ppermute | solution.py:376
  33.1 7.3 %collective-permute-start.13 = (f32[8,48,128]{2,1,0:T(8,128)S(1)}, f32[8,48,128]{2,1,0:T(8,128)S(1)}, u32[]{:S(2)}, u32[]{:S(2)}) collective-permute-start(f32[8,48,128]{2,1,0:T(8,128)S(1)} %get-tuple-element.44), channel_id=1, source_target_pairs={{0,64},{8,72},{16,80},{24,88},{32,96},{40,104},{48,112},{56,120},{... | collective-permute-start | bytes 589832 | tf_op jit(solution)/shard_map/ppermute | solution.py:376
  33.6 9.6 %collective-permute-start.14 = (f32[8,48,128]{2,1,0:T(8,128)S(1)}, f32[8,48,128]{2,1,0:T(8,128)S(1)}, u32[]{:S(2)}, u32[]{:S(2)}) collective-permute-start(f32[8,48,128]{2,1,0:T(8,128)S(1)} %get-tuple-element.45), channel_id=1, source_target_pairs={{0,128},{8,136},{16,144},{24,152},{32,160},{40,168},{48,176},{56,1... | collective-permute-start | bytes 589832 | tf_op jit(solution)/shard_map/ppermute | solution.py:376
  35.4 7.7 %collective-permute-start.15 = (f32[8,48,128]{2,1,0:T(8,128)S(1)}, f32[8,48,128]{2,1,0:T(8,128)S(1)}, u32[]{:S(2)}, u32[]{:S(2)}) collective-permute-start(f32[8,48,128]{2,1,0:T(8,128)S(1)} %get-tuple-element.46), channel_id=1, source_target_pairs={{0,192},{8,200},{16,208},{24,216},{32,224},{40,232},{48,240},{56,2... | collective-permute-start | bytes 589832 | tf_op jit(solution)/shard_map/ppermute | solution.py:376
  37.3 11.8 %collective-permute-start.7 = (f32[8,40,128]{2,1,0:T(8,128)S(1)}, f32[8,40,128]{2,1,0:T(8,128)S(1)}, u32[]{:S(2)}, u32[]{:S(2)}) collective-permute-start(f32[8,40,128]{2,1,0:T(8,128)S(1)} %shard_map.94), channel_id=1, source_target_pairs={{0,48},{8,56},{16,0},{24,8},{32,16},{40,24},{48,32},{56,40},{64,11... | collective-permute-start | bytes 491528 | tf_op jit(solution)/shard_map/ppermute | solution.py:376
  40.2 11.1 %collective-permute-start.6 = (f32[8,40,128]{2,1,0:T(8,128)S(1)}, f32[8,40,128]{2,1,0:T(8,128)S(1)}, u32[]{:S(2)}, u32[]{:S(2)}) collective-permute-start(f32[8,40,128]{2,1,0:T(8,128)S(1)} %shard_map.93), channel_id=1, source_target_pairs={{0,16},{8,24},{16,32},{24,40},{32,48},{40,56},{48,0},{56,8},{64,80... | collective-permute-start | bytes 491528 | tf_op jit(solution)/shard_map/ppermute | solution.py:376
  40.5 8.7 %collective-permute-start.5 = (f32[4,40,128]{2,1,0:T(8,128)S(1)}, f32[4,40,128]{2,1,0:T(8,128)S(1)}, u32[]{:S(2)}, u32[]{:S(2)}) collective-permute-start(f32[4,40,128]{2,1,0:T(8,128)S(1)} %get-tuple-element.37), channel_id=1, source_target_pairs={{0,32},{8,40},{16,48},{24,56},{32,0},{40,8},{48,16},{56,24},{64,96... | collective-permute-start | bytes 245768 | tf_op jit(solution)/shard_map/ppermute | solution.py:376
  43.2 25.4 %copy-start.4 = (f32[136]{0:T(256)S(1)}, f32[136]{0:T(256)}, u32[]{:S(2)}) copy-start(f32[136]{0:T(256)} %param.16) | copy-start | bytes 1636
  43.2 33.5 %copy-start = (f32[136,136]{1,0:T(8,128)S(1)}, f32[136,136]{1,0:T(8,128)}, u32[]{:S(2)}) copy-start(f32[136,136]{1,0:T(8,128)} %refs_2_.1) | copy-start | bytes 221956
  43.2 33.5 %copy-start.1 = (f32[136,136]{1,0:T(8,128)S(1)}, f32[136,136]{1,0:T(8,128)}, u32[]{:S(2)}) copy-start(f32[136,136]{1,0:T(8,128)} %refs_3_.1) | copy-start | bytes 221956
  43.2 33.5 %copy-start.2 = (f32[136,136]{1,0:T(8,128)S(1)}, f32[136,136]{1,0:T(8,128)}, u32[]{:S(2)}) copy-start(f32[136,136]{1,0:T(8,128)} %refs_4_.1) | copy-start | bytes 221956
  43.2 33.5 %copy-start.3 = (s32[24]{0:T(128)S(1)}, s32[24]{0:T(128)}, u32[]{:S(2)}) copy-start(s32[24]{0:T(128)} %refs_1_.1) | copy-start | bytes 292
  55.5 10.2 %collective-permute-start.16 = (f32[176,128]{1,0:T(8,128)S(1)}, f32[176,128]{1,0:T(8,128)S(1)}, u32[]{:S(2)}, u32[]{:S(2)}) collective-permute-start(f32[176,128]{1,0:T(8,128)S(1)} %get-tuple-element.50), channel_id=1, source_target_pairs={{0,1},{1,0},{2,3},{3,2},{4,5},{5,4},{6,7},{7,6},{8,9},{9,8},{10,11... | collective-permute-start | bytes 270344 | tf_op jit(solution)/shard_map/ppermute | solution.py:443
  60.6 7.5 %collective-permute-start.17 = (f32[176,128]{1,0:T(8,128)S(1)}, f32[176,128]{1,0:T(8,128)S(1)}, u32[]{:S(2)}, u32[]{:S(2)}) collective-permute-start(f32[176,128]{1,0:T(8,128)S(1)} %get-tuple-element.51), channel_id=1, source_target_pairs={{0,2},{1,3},{2,0},{3,1},{4,6},{5,7},{6,4},{7,5},{8,10},{9,11},{10,... | collective-permute-start | bytes 270344 | tf_op jit(solution)/shard_map/ppermute | solution.py:443
  61.8 6.9 %collective-permute-start.18 = (f32[176,128]{1,0:T(8,128)S(1)}, f32[176,128]{1,0:T(8,128)S(1)}, u32[]{:S(2)}, u32[]{:S(2)}) collective-permute-start(f32[176,128]{1,0:T(8,128)S(1)} %get-tuple-element.52), channel_id=1, source_target_pairs={{0,3},{1,2},{2,1},{3,0},{4,7},{5,6},{6,5},{7,4},{8,11},{9,10},{10,... | collective-permute-start | bytes 270344 | tf_op jit(solution)/shard_map/ppermute | solution.py:443
  62.4 8.4 %collective-permute-start.19 = (f32[176,128]{1,0:T(8,128)S(1)}, f32[176,128]{1,0:T(8,128)S(1)}, u32[]{:S(2)}, u32[]{:S(2)}) collective-permute-start(f32[176,128]{1,0:T(8,128)S(1)} %get-tuple-element.53), channel_id=1, source_target_pairs={{0,4},{1,5},{2,6},{3,7},{4,0},{5,1},{6,2},{7,3},{8,12},{9,13},{10,... | collective-permute-start | bytes 270344 | tf_op jit(solution)/shard_map/ppermute | solution.py:443
  65.1 8.0 %collective-permute-start.20 = (f32[176,128]{1,0:T(8,128)S(1)}, f32[176,128]{1,0:T(8,128)S(1)}, u32[]{:S(2)}, u32[]{:S(2)}) collective-permute-start(f32[176,128]{1,0:T(8,128)S(1)} %get-tuple-element.54), channel_id=1, source_target_pairs={{0,5},{1,4},{2,7},{3,6},{4,1},{5,0},{6,3},{7,2},{8,13},{9,12},{10,... | collective-permute-start | bytes 270344 | tf_op jit(solution)/shard_map/ppermute | solution.py:443
  65.6 9.0 %collective-permute-start.21 = (f32[176,128]{1,0:T(8,128)S(1)}, f32[176,128]{1,0:T(8,128)S(1)}, u32[]{:S(2)}, u32[]{:S(2)}) collective-permute-start(f32[176,128]{1,0:T(8,128)S(1)} %get-tuple-element.55), channel_id=1, source_target_pairs={{0,6},{1,7},{2,4},{3,5},{4,2},{5,3},{6,0},{7,1},{8,14},{9,15},{10,... | collective-permute-start | bytes 270344 | tf_op jit(solution)/shard_map/ppermute | solution.py:443
  68.1 8.5 %collective-permute-start.22 = (f32[176,128]{1,0:T(8,128)S(1)}, f32[176,128]{1,0:T(8,128)S(1)}, u32[]{:S(2)}, u32[]{:S(2)}) collective-permute-start(f32[176,128]{1,0:T(8,128)S(1)} %get-tuple-element.56), channel_id=1, source_target_pairs={{0,7},{1,6},{2,5},{3,4},{4,3},{5,2},{6,1},{7,0},{8,15},{9,14},{10,... | collective-permute-start | bytes 270344 | tf_op jit(solution)/shard_map/ppermute | solution.py:443

commit v5 on v4

--- a/solution.py
+++ b/solution.py
@@ -250,10 +250,10 @@
     for p in range(2):
         rhsb[p] = rhs[p].astype(BF16)
 
-    @pl.loop(0, count)
-    def _(n):
-        if wide:
-
+    if wide:
+
+        @pl.loop(0, count)
+        def _(n):
             @pl.when(n + AHEAD < count)
             def _():
                 read(n + AHEAD).start()
@@ -262,11 +262,21 @@
             high, low = split(table[n])
             keep[n, 0] = high
             keep[n, 1] = low
-        p = n // each
-        at = pl.multiple_of((n - p * each) * step, 8)
-        both = keep[n].reshape(2 * step, keep.shape[3])
-        o = jnp.dot(both, rhsb[p], preferred_element_type=F32)
-        res[p, pl.ds(at, step), :] = o[:step] + o[step:]
+            p = n // each
+            at = pl.multiple_of((n - p * each) * step, 8)
+            both = keep[n].reshape(2 * step, keep.shape[3])
+            o = jnp.dot(both, rhsb[p], preferred_element_type=F32)
+            res[p, pl.ds(at, step), :] = o[:step] + o[step:]
+
+    else:
+
+        @pl.loop(0, 2)
+        def _(p):
+            half_table = keep[pl.ds(each * p, each)].reshape(each * 2 * step, keep.shape[3])
+            o = jnp.dot(half_table, rhsb[p], preferred_element_type=F32)
+            for n in range(each):
+                at = 2 * step * n
+                res[p, step * n : step * n + step, :] = o[at : at + step] + o[at + step : at + 2 * step]
 
     for r in range(8):
         mine = pl.ds(pl.multiple_of(80 * (me ^ r), 8), 80)

time: 80 us -> 79.6 us (level)
  no operation moved by 1% of the time
where the time goes in v5:
time: 79.6 us; the launch traced here: 79.4 us
  starting transfers between devices  42.5 us (53%)
  Pallas kernels  18.7 us (23%)
  waiting for transfers between devices  17.8 us (22%)
    ppermute x16, starting transfers between devices, shift(): return lax.ppermute(v, axis, [(i, move(i)) for i in range(size)])  29.3 us
    ppermute x7, starting transfers between devices, on_device(): lax.ppermute(local[r], 'lev', [(i, i ^ r) for i in range(members)])  13.1 us
    ppermute x16, waiting for transfers between devices, shift(): return lax.ppermute(v, axis, [(i, move(i)) for i in range(size)])  9.91 us
    pallas_call x2, Pallas kernels, legendre(): pl.pallas_call(functools.partial(legendre_kernel, places, wide), out_shap...  9.71 us
    ppermute x7, waiting for transfers between devices, on_device(): lax.ppermute(local[r], 'lev', [(i, i ^ r) for i in range(members)])  7.92 us
    pallas_call x2, Pallas kernels, pack(): pl.pallas_call(lambda *r: pack_kernel(stride, first, sends, *r), out_shap...  5.78 us
    pallas_call x1, Pallas kernels, vertical(): pl.pallas_call(lambda *refs: vertical_kernel(stride, *refs), out_shape=ja...  3.11 us
  transfers between devices with their start and end apart: 23, of which 9 were waited for; matrix products, arithmetic and copies ran while one was open for 0% of the time, Pallas kernels for 11%

profile of v5, /device:TPU:1, one launch (start us, length us, event | category | flops | bytes accessed | tf_op | source)
XLA Modules:
  0.0 79.4 jit_solution(11871299812419809154)
XLA Ops:
  0.0 0.1 pad_add_fusion.r_0_.where_ref.refs_0_
  0.1 2.9 %shard_map.95 = (f32[8,48,128]{2,1,0:T(8,128)S(1)}, f32[8,48,128]{2,1,0:T(8,128)S(1)}, f32[4,48,128]{2,1,0:T(8,128)S(1)}, f32[4,48,128]{2,1,0:T(8,128)S(1)}, f32...) custom-call(s32[2]{0:T(128)S(1)} %pad_add_fusion.r_0_.where_ref.refs_0_, s32[24]{0:T(128)} %refs_1_.1, ...), custom_call_target="tpu_custom_call" | custom-call | tf_op jit(solution)/shard_map/pallas_call | solution.py:146
  3.0 2.5 %collective-permute-start.8 = (f32[8,48,128]{2,1,0:T(8,128)S(1)}, f32[8,48,128]{2,1,0:T(8,128)S(1)}, u32[]{:S(2)}, u32[]{:S(2)}) collective-permute-start(f32[8,48,128]{2,1,0:T(8,128)S(1)} %get-tuple-element.38), channel_id=1, source_target_pairs={{0,8},{8,16},{16,24},{24,32},{32,40},{40,48},{48,56},{56,0},{64,72... | collective-permute-start | bytes 589832 | tf_op jit(solution)/shard_map/ppermute | solution.py:386
  5.5 4.0 %collective-permute-start.9 = (f32[8,48,128]{2,1,0:T(8,128)S(1)}, f32[8,48,128]{2,1,0:T(8,128)S(1)}, u32[]{:S(2)}, u32[]{:S(2)}) collective-permute-start(f32[8,48,128]{2,1,0:T(8,128)S(1)} %get-tuple-element.39), channel_id=1, source_target_pairs={{0,56},{8,0},{16,8},{24,16},{32,24},{40,32},{48,40},{56,48},{64,12... | collective-permute-start | bytes 589832 | tf_op jit(solution)/shard_map/ppermute | solution.py:386
  9.6 2.9 %shard_map.91 = (f32[8,40,128]{2,1,0:T(8,128)S(1)}, f32[8,40,128]{2,1,0:T(8,128)S(1)}, f32[8,40,128]{2,1,0:T(8,128)S(1)}, f32[8,40,128]{2,1,0:T(8,128)S(1)}) custom-call(s32[2]{0:T(128)S(1)} %pad_add_fusion.r_0_.where_ref.refs_0_, s32[24]{0:T(128)} %refs_1_.1, s32[20,128]{1,0:T(8,128)} %bitcast.12, f32[1,80]{1,0:T(1,128)} %bitcast.14, f32[24,136,80]{2,1,0:T(8,128)} %bitcast.9), custom_call_target="tpu_custom_call" | custom-call | tf_op jit(solution)/shard_map/pallas_call | solution.py:146
  12.4 1.4 %collective-permute-start = (f32[8,40,128]{2,1,0:T(8,128)S(1)}, f32[8,40,128]{2,1,0:T(8,128)S(1)}, u32[]{:S(2)}, u32[]{:S(2)}) collective-permute-start(f32[8,40,128]{2,1,0:T(8,128)S(1)} %get-tuple-element.32), channel_id=1, source_target_pairs={{0,64},{8,72},{16,80},{24,88},{32,96},{40,104},{48,112},{56,120},{... | collective-permute-start | bytes 491528 | tf_op jit(solution)/shard_map/ppermute | solution.py:386
  13.8 2.6 %collective-permute-start.1 = (f32[8,40,128]{2,1,0:T(8,128)S(1)}, f32[8,40,128]{2,1,0:T(8,128)S(1)}, u32[]{:S(2)}, u32[]{:S(2)}) collective-permute-start(f32[8,40,128]{2,1,0:T(8,128)S(1)} %get-tuple-element.33), channel_id=1, source_target_pairs={{0,128},{8,136},{16,144},{24,152},{32,160},{40,168},{48,176},{56,1... | collective-permute-start | bytes 491528 | tf_op jit(solution)/shard_map/ppermute | solution.py:386
  16.4 1.1 %collective-permute-start.2 = (f32[8,40,128]{2,1,0:T(8,128)S(1)}, f32[8,40,128]{2,1,0:T(8,128)S(1)}, u32[]{:S(2)}, u32[]{:S(2)}) collective-permute-start(f32[8,40,128]{2,1,0:T(8,128)S(1)} %get-tuple-element.34), channel_id=1, source_target_pairs={{0,192},{8,200},{16,208},{24,216},{32,224},{40,232},{48,240},{56,2... | collective-permute-start | bytes 491528 | tf_op jit(solution)/shard_map/ppermute | solution.py:386
  17.5 0.0 collective-permute-done.8.refs_1_.refs_0_
  17.5 0.1 collective-permute-start.11
  17.6 0.0 collective-permute-done.9.refs_1_
  17.6 3.6 %collective-permute-start.12 = (f32[8,48,128]{2,1,0:T(8,128)S(1)}, f32[8,48,128]{2,1,0:T(8,128)S(1)}, u32[]{:S(2)}, u32[]{:S(2)}) collective-permute-start(f32[8,48,128]{2,1,0:T(8,128)S(1)} %shard_map.97), channel_id=1, source_target_pairs={{0,48},{8,56},{16,0},{24,8},{32,16},{40,24},{48,32},{56,40},{64,11... | collective-permute-start | bytes 589832 | tf_op jit(solution)/shard_map/ppermute | solution.py:386
  21.3 0.0 collective-permute-done.refs_1_.refs_6_
  21.3 3.9 %collective-permute-start.10 = (f32[4,48,128]{2,1,0:T(8,128)S(1)}, f32[4,48,128]{2,1,0:T(8,128)S(1)}, u32[]{:S(2)}, u32[]{:S(2)}) collective-permute-start(f32[4,48,128]{2,1,0:T(8,128)S(1)} %get-tuple-element.40), channel_id=1, source_target_pairs={{0,32},{8,40},{16,48},{24,56},{32,0},{40,8},{48,16},{56,24},{64,96... | collective-permute-start | bytes 294920 | tf_op jit(solution)/shard_map/ppermute | solution.py:386
  25.2 0.0 collective-permute-done.1.refs_2_.refs_7_
  25.2 0.0 collective-permute-done.2.refs_3_.refs_8_
  25.2 0.1 collective-permute-start.4
  25.3 1.5 %collective-permute-start.3 = (f32[8,40,128]{2,1,0:T(8,128)S(1)}, f32[8,40,128]{2,1,0:T(8,128)S(1)}, u32[]{:S(2)}, u32[]{:S(2)}) collective-permute-start(f32[8,40,128]{2,1,0:T(8,128)S(1)} %get-tuple-element.35), channel_id=1, source_target_pairs={{0,8},{8,16},{16,24},{24,32},{32,40},{40,48},{48,56},{56,0},{64,72... | collective-permute-start | bytes 491528 | tf_op jit(solution)/shard_map/ppermute | solution.py:386
  26.8 4.7 %collective-permute-done.10.refs_2_ = f32[4,48,128]{2,1,0:T(8,128)S(1)} collective-permute-done((f32[4,48,128]{2,1,0:T(8,128)S(1)}, f32[4,48,128]{2,1,0:T(8,128)S(1)}, u32[]{:S(2)}, u32[]{:S(2)}) %collective-permute-start.10) | collective-permute-done | bytes 98336 | tf_op jit(solution)/shard_map/ppermute | solution.py:386
  31.5 0.0 collective-permute-done.11.refs_3_
  31.5 1.6 %collective-permute-done.12.refs_4_ = f32[8,48,128]{2,1,0:T(8,128)S(1)} collective-permute-done((f32[8,48,128]{2,1,0:T(8,128)S(1)}, f32[8,48,128]{2,1,0:T(8,128)S(1)}, u32[]{:S(2)}, u32[]{:S(2)}) %collective-permute-start.12) | collective-permute-done | bytes 196640 | tf_op jit(solution)/shard_map/ppermute | solution.py:386
  33.1 0.5 collective-permute-start.13
  33.6 1.8 %collective-permute-start.14 = (f32[8,48,128]{2,1,0:T(8,128)S(1)}, f32[8,48,128]{2,1,0:T(8,128)S(1)}, u32[]{:S(2)}, u32[]{:S(2)}) collective-permute-start(f32[8,48,128]{2,1,0:T(8,128)S(1)} %get-tuple-element.45), channel_id=1, source_target_pairs={{0,128},{8,136},{16,144},{24,152},{32,160},{40,168},{48,176},{56,1... | collective-permute-start | bytes 589832 | tf_op jit(solution)/shard_map/ppermute | solution.py:386
  35.4 0.7 collective-permute-start.15
  36.1 1.2 %collective-permute-done.4.refs_4_.refs_2_ = f32[8,40,128]{2,1,0:T(8,128)S(1)} collective-permute-done((f32[8,40,128]{2,1,0:T(8,128)S(1)}, f32[8,40,128]{2,1,0:T(8,128)S(1)}, u32[]{:S(2)}, u32[]{:S(2)}) %collective-permute-start.4) | collective-permute-done | bytes 163872 | tf_op jit(solution)/shard_map/ppermute | solution.py:386
  37.3 2.8 %collective-permute-start.7 = (f32[8,40,128]{2,1,0:T(8,128)S(1)}, f32[8,40,128]{2,1,0:T(8,128)S(1)}, u32[]{:S(2)}, u32[]{:S(2)}) collective-permute-start(f32[8,40,128]{2,1,0:T(8,128)S(1)} %shard_map.94), channel_id=1, source_target_pairs={{0,48},{8,56},{16,0},{24,8},{32,16},{40,24},{48,32},{56,40},{64,11... | collective-permute-start | bytes 491528 | tf_op jit(solution)/shard_map/ppermute | solution.py:386
  40.2 0.0 collective-permute-done.3.refs_4_.refs_1_
  40.2 0.3 collective-permute-start.6
  40.4 0.0 collective-permute-done.13.refs_6_
  40.5 2.5 %collective-permute-start.5 = (f32[4,40,128]{2,1,0:T(8,128)S(1)}, f32[4,40,128]{2,1,0:T(8,128)S(1)}, u32[]{:S(2)}, u32[]{:S(2)}) collective-permute-start(f32[4,40,128]{2,1,0:T(8,128)S(1)} %get-tuple-element.37), channel_id=1, source_target_pairs={{0,32},{8,40},{16,48},{24,56},{32,0},{40,8},{48,16},{56,24},{64,96... | collective-permute-start | bytes 245768 | tf_op jit(solution)/shard_map/ppermute | solution.py:386
  42.9 0.2 collective-permute-done.14.refs_7_
  43.2 0.0 collective-permute-done.15.refs_8_
  43.2 0.0 copy-start.4
  43.2 0.0 copy-start
  43.2 0.0 copy-start.1
  43.2 0.0 copy-start.2
  43.2 0.0 copy-start.3
  43.2 5.9 %shard_map.99 = (f32[8,96,128]{2,1,0:T(8,128)S(1)}, bf16[4,2,320,1280]{3,2,1,0:T(8,128)(2,1)S(1)}) custom-call(s32[2]{0:T(128)S(1)} %pad_add_fusion.r_0_.where_ref.refs_0_, f32[8,48,128]{2,1,0:T(8,128)S(1)} %collective-permute-done.8.refs_1_.refs_0_, f32[8,48,128]{2,1,0:T(8,128)S(1)} %collective-permute-done.9.refs_1_, ...), custom_call_target="tpu_custom_call" | custom-call | tf_op jit(solution)/shard_map/pallas_call | solution.py:304
  49.1 0.0 collective-permute-done.5.refs_3_
  49.1 0.0 collective-permute-done.7.refs_5_
  49.1 2.1 %collective-permute-done.6.refs_4_ = f32[8,40,128]{2,1,0:T(8,128)S(1)} collective-permute-done((f32[8,40,128]{2,1,0:T(8,128)S(1)}, f32[8,40,128]{2,1,0:T(8,128)S(1)}, u32[]{:S(2)}, u32[]{:S(2)}) %collective-permute-start.6) | collective-permute-done | bytes 163872 | tf_op jit(solution)/shard_map/ppermute | solution.py:386
  51.3 3.8 %shard_map.100 = (f32[176,128]{1,0:T(8,128)S(1)}, f32[176,128]{1,0:T(8,128)S(1)}, f32[176,128]{1,0:T(8,128)S(1)}, f32[176,128]{1,0:T(8,128)S(1)}, f32[176,128]{1...) custom-call(s32[2]{0:T(128)S(1)} %pad_add_fusion.r_0_.where_ref.refs_0_, ...), custom_call_target="tpu_custom_call" | custom-call | tf_op jit(solution)/shard_map/pallas_call | solution.py:304
  55.1 5.2 %collective-permute-start.16 = (f32[176,128]{1,0:T(8,128)S(1)}, f32[176,128]{1,0:T(8,128)S(1)}, u32[]{:S(2)}, u32[]{:S(2)}) collective-permute-start(f32[176,128]{1,0:T(8,128)S(1)} %get-tuple-element.50), channel_id=1, source_target_pairs={{0,1},{1,0},{2,3},{3,2},{4,5},{5,4},{6,7},{7,6},{8,9},{9,8},{10,11... | collective-permute-start | bytes 270344 | tf_op jit(solution)/shard_map/ppermute | solution.py:453
  60.3 1.2 %collective-permute-start.17 = (f32[176,128]{1,0:T(8,128)S(1)}, f32[176,128]{1,0:T(8,128)S(1)}, u32[]{:S(2)}, u32[]{:S(2)}) collective-permute-start(f32[176,128]{1,0:T(8,128)S(1)} %get-tuple-element.51), channel_id=1, source_target_pairs={{0,2},{1,3},{2,0},{3,1},{4,6},{5,7},{6,4},{7,5},{8,10},{9,11},{10,... | collective-permute-start | bytes 270344 | tf_op jit(solution)/shard_map/ppermute | solution.py:453
  61.5 0.5 collective-permute-start.18
  62.0 2.7 %collective-permute-start.19 = (f32[176,128]{1,0:T(8,128)S(1)}, f32[176,128]{1,0:T(8,128)S(1)}, u32[]{:S(2)}, u32[]{:S(2)}) collective-permute-start(f32[176,128]{1,0:T(8,128)S(1)} %get-tuple-element.53), channel_id=1, source_target_pairs={{0,4},{1,5},{2,6},{3,7},{4,0},{5,1},{6,2},{7,3},{8,12},{9,13},{10,... | collective-permute-start | bytes 270344 | tf_op jit(solution)/shard_map/ppermute | solution.py:453
  64.7 0.5 collective-permute-start.20
  65.3 0.0 collective-permute-done.16.refs_7_
  65.3 2.5 %collective-permute-start.21 = (f32[176,128]{1,0:T(8,128)S(1)}, f32[176,128]{1,0:T(8,128)S(1)}, u32[]{:S(2)}, u32[]{:S(2)}) collective-permute-start(f32[176,128]{1,0:T(8,128)S(1)} %get-tuple-element.55), channel_id=1, source_target_pairs={{0,6},{1,7},{2,4},{3,5},{4,2},{5,3},{6,0},{7,1},{8,14},{9,15},{10,... | collective-permute-start | bytes 270344 | tf_op jit(solution)/shard_map/ppermute | solution.py:453
  67.7 0.0 collective-permute-done.17.refs_8_
  67.7 0.5 collective-permute-start.22
  68.2 0.0 copy-done.4
  68.2 0.1 copy.10.refs_5_
  68.3 0.0 collective-permute-done.18.refs_9_
  68.3 2.1 %collective-permute-done.19.refs_10_ = f32[176,128]{1,0:T(8,128)S(1)} collective-permute-done((f32[176,128]{1,0:T(8,128)S(1)}, f32[176,128]{1,0:T(8,128)S(1)}, u32[]{:S(2)}, u32[]{:S(2)}) %collective-permute-start.19) | collective-permute-done | bytes 90144 | tf_op jit(solution)/shard_map/ppermute | solution.py:453
  70.4 2.3 %collective-permute-done.20.refs_11_ = f32[176,128]{1,0:T(8,128)S(1)} collective-permute-done((f32[176,128]{1,0:T(8,128)S(1)}, f32[176,128]{1,0:T(8,128)S(1)}, u32[]{:S(2)}, u32[]{:S(2)}) %collective-permute-start.20) | collective-permute-done | bytes 90144 | tf_op jit(solution)/shard_map/ppermute | solution.py:453
  72.7 1.6 %collective-permute-done.21.refs_12_ = f32[176,128]{1,0:T(8,128)S(1)} collective-permute-done((f32[176,128]{1,0:T(8,128)S(1)}, f32[176,128]{1,0:T(8,128)S(1)}, u32[]{:S(2)}, u32[]{:S(2)}) %collective-permute-start.21) | collective-permute-done | bytes 90144 | tf_op jit(solution)/shard_map/ppermute | solution.py:453
  74.3 1.9 %collective-permute-done.22.refs_13_ = f32[176,128]{1,0:T(8,128)S(1)} collective-permute-done((f32[176,128]{1,0:T(8,128)S(1)}, f32[176,128]{1,0:T(8,128)S(1)}, u32[]{:S(2)}, u32[]{:S(2)}) %collective-permute-start.22) | collective-permute-done | bytes 90144 | tf_op jit(solution)/shard_map/ppermute | solution.py:453
  76.3 0.0 copy-done
  76.3 0.0 copy-done.1
  76.3 0.0 copy-done.2
  76.3 0.0 copy-done.3
  76.3 3.1 %vertical.1 = f32[2,80,1088]{2,1,0:T(8,128)} custom-call(s32[2]{0:T(128)S(1)} %pad_add_fusion.r_0_.where_ref.refs_0_, s32[24]{0:T(128)S(1)} %copy-done.3, f32[136,136]{1,0:T(8,128)S(1)} %copy-done, f32[136,136]{1,0:T(8,128)S(1)} %copy-done.1, f32[136,136]{1,0:T(8,128)S(1)} %copy-done.2, f32[136,1]{1,0:T(8,128)S(1)} %copy.10.refs_5_, ...), custom_call_target="tpu_custom_call" | custom-call | tf_op jit(solution)/shard_map/vertical/pallas_call | solution.py:374
  (6 shorter events, 0.1 us)
Async XLA Ops:
  3.0 14.5 %collective-permute-start.8 = (f32[8,48,128]{2,1,0:T(8,128)S(1)}, f32[8,48,128]{2,1,0:T(8,128)S(1)}, u32[]{:S(2)}, u32[]{:S(2)}) collective-permute-start(f32[8,48,128]{2,1,0:T(8,128)S(1)} %get-tuple-element.38), channel_id=1, source_target_pairs={{0,8},{8,16},{16,24},{24,32},{32,40},{40,48},{48,56},{56,0},{64,72... | collective-permute-start | bytes 589832 | tf_op jit(solution)/shard_map/ppermute | solution.py:386
  5.5 12.1 %collective-permute-start.9 = (f32[8,48,128]{2,1,0:T(8,128)S(1)}, f32[8,48,128]{2,1,0:T(8,128)S(1)}, u32[]{:S(2)}, u32[]{:S(2)}) collective-permute-start(f32[8,48,128]{2,1,0:T(8,128)S(1)} %get-tuple-element.39), channel_id=1, source_target_pairs={{0,56},{8,0},{16,8},{24,16},{32,24},{40,32},{48,40},{56,48},{64,12... | collective-permute-start | bytes 589832 | tf_op jit(solution)/shard_map/ppermute | solution.py:386
  12.4 8.8 %collective-permute-start = (f32[8,40,128]{2,1,0:T(8,128)S(1)}, f32[8,40,128]{2,1,0:T(8,128)S(1)}, u32[]{:S(2)}, u32[]{:S(2)}) collective-permute-start(f32[8,40,128]{2,1,0:T(8,128)S(1)} %get-tuple-element.32), channel_id=1, source_target_pairs={{0,64},{8,72},{16,80},{24,88},{32,96},{40,104},{48,112},{56,120},{... | collective-permute-start | bytes 491528 | tf_op jit(solution)/shard_map/ppermute | solution.py:386
  13.8 11.4 %collective-permute-start.1 = (f32[8,40,128]{2,1,0:T(8,128)S(1)}, f32[8,40,128]{2,1,0:T(8,128)S(1)}, u32[]{:S(2)}, u32[]{:S(2)}) collective-permute-start(f32[8,40,128]{2,1,0:T(8,128)S(1)} %get-tuple-element.33), channel_id=1, source_target_pairs={{0,128},{8,136},{16,144},{24,152},{32,160},{40,168},{48,176},{56,1... | collective-permute-start | bytes 491528 | tf_op jit(solution)/shard_map/ppermute | solution.py:386
  16.4 8.8 %collective-permute-start.2 = (f32[8,40,128]{2,1,0:T(8,128)S(1)}, f32[8,40,128]{2,1,0:T(8,128)S(1)}, u32[]{:S(2)}, u32[]{:S(2)}) collective-permute-start(f32[8,40,128]{2,1,0:T(8,128)S(1)} %get-tuple-element.34), channel_id=1, source_target_pairs={{0,192},{8,200},{16,208},{24,216},{32,224},{40,232},{48,240},{56,2... | collective-permute-start | bytes 491528 | tf_op jit(solution)/shard_map/ppermute | solution.py:386
  17.5 13.9 %collective-permute-start.11 = (f32[8,48,128]{2,1,0:T(8,128)S(1)}, f32[8,48,128]{2,1,0:T(8,128)S(1)}, u32[]{:S(2)}, u32[]{:S(2)}) collective-permute-start(f32[8,48,128]{2,1,0:T(8,128)S(1)} %shard_map.96), channel_id=1, source_target_pairs={{0,16},{8,24},{16,32},{24,40},{32,48},{40,56},{48,0},{56,8},{64,80... | collective-permute-start | bytes 589832 | tf_op jit(solution)/shard_map/ppermute | solution.py:386
  17.6 15.4 %collective-permute-start.12 = (f32[8,48,128]{2,1,0:T(8,128)S(1)}, f32[8,48,128]{2,1,0:T(8,128)S(1)}, u32[]{:S(2)}, u32[]{:S(2)}) collective-permute-start(f32[8,48,128]{2,1,0:T(8,128)S(1)} %shard_map.97), channel_id=1, source_target_pairs={{0,48},{8,56},{16,0},{24,8},{32,16},{40,24},{48,32},{56,40},{64,11... | collective-permute-start | bytes 589832 | tf_op jit(solution)/shard_map/ppermute | solution.py:386
  21.3 10.2 %collective-permute-start.10 = (f32[4,48,128]{2,1,0:T(8,128)S(1)}, f32[4,48,128]{2,1,0:T(8,128)S(1)}, u32[]{:S(2)}, u32[]{:S(2)}) collective-permute-start(f32[4,48,128]{2,1,0:T(8,128)S(1)} %get-tuple-element.40), channel_id=1, source_target_pairs={{0,32},{8,40},{16,48},{24,56},{32,0},{40,8},{48,16},{56,24},{64,96... | collective-permute-start | bytes 294920 | tf_op jit(solution)/shard_map/ppermute | solution.py:386
  25.2 12.1 %collective-permute-start.4 = (f32[8,40,128]{2,1,0:T(8,128)S(1)}, f32[8,40,128]{2,1,0:T(8,128)S(1)}, u32[]{:S(2)}, u32[]{:S(2)}) collective-permute-start(f32[8,40,128]{2,1,0:T(8,128)S(1)} %get-tuple-element.36), channel_id=1, source_target_pairs={{0,56},{8,0},{16,8},{24,16},{32,24},{40,32},{48,40},{56,48},{64,12... | collective-permute-start | bytes 491528 | tf_op jit(solution)/shard_map/ppermute | solution.py:386
  25.3 14.8 %collective-permute-start.3 = (f32[8,40,128]{2,1,0:T(8,128)S(1)}, f32[8,40,128]{2,1,0:T(8,128)S(1)}, u32[]{:S(2)}, u32[]{:S(2)}) collective-permute-start(f32[8,40,128]{2,1,0:T(8,128)S(1)} %get-tuple-element.35), channel_id=1, source_target_pairs={{0,8},{8,16},{16,24},{24,32},{32,40},{40,48},{48,56},{56,0},{64,72... | collective-permute-start | bytes 491528 | tf_op jit(solution)/shard_map/ppermute | solution.py:386
  33.1 7.3 %collective-permute-start.13 = (f32[8,48,128]{2,1,0:T(8,128)S(1)}, f32[8,48,128]{2,1,0:T(8,128)S(1)}, u32[]{:S(2)}, u32[]{:S(2)}) collective-permute-start(f32[8,48,128]{2,1,0:T(8,128)S(1)} %get-tuple-element.44), channel_id=1, source_target_pairs={{0,64},{8,72},{16,80},{24,88},{32,96},{40,104},{48,112},{56,120},{... | collective-permute-start | bytes 589832 | tf_op jit(solution)/shard_map/ppermute | solution.py:386
  33.6 9.6 %collective-permute-start.14 = (f32[8,48,128]{2,1,0:T(8,128)S(1)}, f32[8,48,128]{2,1,0:T(8,128)S(1)}, u32[]{:S(2)}, u32[]{:S(2)}) collective-permute-start(f32[8,48,128]{2,1,0:T(8,128)S(1)} %get-tuple-element.45), channel_id=1, source_target_pairs={{0,128},{8,136},{16,144},{24,152},{32,160},{40,168},{48,176},{56,1... | collective-permute-start | bytes 589832 | tf_op jit(solution)/shard_map/ppermute | solution.py:386
  35.4 7.7 %collective-permute-start.15 = (f32[8,48,128]{2,1,0:T(8,128)S(1)}, f32[8,48,128]{2,1,0:T(8,128)S(1)}, u32[]{:S(2)}, u32[]{:S(2)}) collective-permute-start(f32[8,48,128]{2,1,0:T(8,128)S(1)} %get-tuple-element.46), channel_id=1, source_target_pairs={{0,192},{8,200},{16,208},{24,216},{32,224},{40,232},{48,240},{56,2... | collective-permute-start | bytes 589832 | tf_op jit(solution)/shard_map/ppermute | solution.py:386
  37.3 11.8 %collective-permute-start.7 = (f32[8,40,128]{2,1,0:T(8,128)S(1)}, f32[8,40,128]{2,1,0:T(8,128)S(1)}, u32[]{:S(2)}, u32[]{:S(2)}) collective-permute-start(f32[8,40,128]{2,1,0:T(8,128)S(1)} %shard_map.94), channel_id=1, source_target_pairs={{0,48},{8,56},{16,0},{24,8},{32,16},{40,24},{48,32},{56,40},{64,11... | collective-permute-start | bytes 491528 | tf_op jit(solution)/shard_map/ppermute | solution.py:386
  40.2 11.1 %collective-permute-start.6 = (f32[8,40,128]{2,1,0:T(8,128)S(1)}, f32[8,40,128]{2,1,0:T(8,128)S(1)}, u32[]{:S(2)}, u32[]{:S(2)}) collective-permute-start(f32[8,40,128]{2,1,0:T(8,128)S(1)} %shard_map.93), channel_id=1, source_target_pairs={{0,16},{8,24},{16,32},{24,40},{32,48},{40,56},{48,0},{56,8},{64,80... | collective-permute-start | bytes 491528 | tf_op jit(solution)/shard_map/ppermute | solution.py:386
  40.5 8.7 %collective-permute-start.5 = (f32[4,40,128]{2,1,0:T(8,128)S(1)}, f32[4,40,128]{2,1,0:T(8,128)S(1)}, u32[]{:S(2)}, u32[]{:S(2)}) collective-permute-start(f32[4,40,128]{2,1,0:T(8,128)S(1)} %get-tuple-element.37), channel_id=1, source_target_pairs={{0,32},{8,40},{16,48},{24,56},{32,0},{40,8},{48,16},{56,24},{64,96... | collective-permute-start | bytes 245768 | tf_op jit(solution)/shard_map/ppermute | solution.py:386
  43.2 25.1 %copy-start.4 = (f32[136]{0:T(256)S(1)}, f32[136]{0:T(256)}, u32[]{:S(2)}) copy-start(f32[136]{0:T(256)} %param.16) | copy-start | bytes 1636
  43.2 33.1 %copy-start = (f32[136,136]{1,0:T(8,128)S(1)}, f32[136,136]{1,0:T(8,128)}, u32[]{:S(2)}) copy-start(f32[136,136]{1,0:T(8,128)} %refs_2_.1) | copy-start | bytes 221956
  43.2 33.1 %copy-start.1 = (f32[136,136]{1,0:T(8,128)S(1)}, f32[136,136]{1,0:T(8,128)}, u32[]{:S(2)}) copy-start(f32[136,136]{1,0:T(8,128)} %refs_3_.1) | copy-start | bytes 221956
  43.2 33.1 %copy-start.2 = (f32[136,136]{1,0:T(8,128)S(1)}, f32[136,136]{1,0:T(8,128)}, u32[]{:S(2)}) copy-start(f32[136,136]{1,0:T(8,128)} %refs_4_.1) | copy-start | bytes 221956
  43.2 33.1 %copy-start.3 = (s32[24]{0:T(128)S(1)}, s32[24]{0:T(128)}, u32[]{:S(2)}) copy-start(s32[24]{0:T(128)} %refs_1_.1) | copy-start | bytes 292
  55.1 10.2 %collective-permute-start.16 = (f32[176,128]{1,0:T(8,128)S(1)}, f32[176,128]{1,0:T(8,128)S(1)}, u32[]{:S(2)}, u32[]{:S(2)}) collective-permute-start(f32[176,128]{1,0:T(8,128)S(1)} %get-tuple-element.50), channel_id=1, source_target_pairs={{0,1},{1,0},{2,3},{3,2},{4,5},{5,4},{6,7},{7,6},{8,9},{9,8},{10,11... | collective-permute-start | bytes 270344 | tf_op jit(solution)/shard_map/ppermute | solution.py:453
  60.3 7.5 %collective-permute-start.17 = (f32[176,128]{1,0:T(8,128)S(1)}, f32[176,128]{1,0:T(8,128)S(1)}, u32[]{:S(2)}, u32[]{:S(2)}) collective-permute-start(f32[176,128]{1,0:T(8,128)S(1)} %get-tuple-element.51), channel_id=1, source_target_pairs={{0,2},{1,3},{2,0},{3,1},{4,6},{5,7},{6,4},{7,5},{8,10},{9,11},{10,... | collective-permute-start | bytes 270344 | tf_op jit(solution)/shard_map/ppermute | solution.py:453
  61.5 6.9 %collective-permute-start.18 = (f32[176,128]{1,0:T(8,128)S(1)}, f32[176,128]{1,0:T(8,128)S(1)}, u32[]{:S(2)}, u32[]{:S(2)}) collective-permute-start(f32[176,128]{1,0:T(8,128)S(1)} %get-tuple-element.52), channel_id=1, source_target_pairs={{0,3},{1,2},{2,1},{3,0},{4,7},{5,6},{6,5},{7,4},{8,11},{9,10},{10,... | collective-permute-start | bytes 270344 | tf_op jit(solution)/shard_map/ppermute | solution.py:453
  62.0 8.4 %collective-permute-start.19 = (f32[176,128]{1,0:T(8,128)S(1)}, f32[176,128]{1,0:T(8,128)S(1)}, u32[]{:S(2)}, u32[]{:S(2)}) collective-permute-start(f32[176,128]{1,0:T(8,128)S(1)} %get-tuple-element.53), channel_id=1, source_target_pairs={{0,4},{1,5},{2,6},{3,7},{4,0},{5,1},{6,2},{7,3},{8,12},{9,13},{10,... | collective-permute-start | bytes 270344 | tf_op jit(solution)/shard_map/ppermute | solution.py:453
  64.7 8.0 %collective-permute-start.20 = (f32[176,128]{1,0:T(8,128)S(1)}, f32[176,128]{1,0:T(8,128)S(1)}, u32[]{:S(2)}, u32[]{:S(2)}) collective-permute-start(f32[176,128]{1,0:T(8,128)S(1)} %get-tuple-element.54), channel_id=1, source_target_pairs={{0,5},{1,4},{2,7},{3,6},{4,1},{5,0},{6,3},{7,2},{8,13},{9,12},{10,... | collective-permute-start | bytes 270344 | tf_op jit(solution)/shard_map/ppermute | solution.py:453
  65.3 9.1 %collective-permute-start.21 = (f32[176,128]{1,0:T(8,128)S(1)}, f32[176,128]{1,0:T(8,128)S(1)}, u32[]{:S(2)}, u32[]{:S(2)}) collective-permute-start(f32[176,128]{1,0:T(8,128)S(1)} %get-tuple-element.55), channel_id=1, source_target_pairs={{0,6},{1,7},{2,4},{3,5},{4,2},{5,3},{6,0},{7,1},{8,14},{9,15},{10,... | collective-permute-start | bytes 270344 | tf_op jit(solution)/shard_map/ppermute | solution.py:453
  67.7 8.5 %collective-permute-start.22 = (f32[176,128]{1,0:T(8,128)S(1)}, f32[176,128]{1,0:T(8,128)S(1)}, u32[]{:S(2)}, u32[]{:S(2)}) collective-permute-start(f32[176,128]{1,0:T(8,128)S(1)} %get-tuple-element.56), channel_id=1, source_target_pairs={{0,7},{1,6},{2,5},{3,4},{4,3},{5,2},{6,1},{7,0},{8,15},{9,14},{10,... | collective-permute-start | bytes 270344 | tf_op jit(solution)/shard_map/ppermute | solution.py:453
